TPU v7x, 32 devices: a whole 2x2x4 slice. The times are simulated.
32 devices in a mesh: img: 16 (over z, x, core), seq: 2 (over y).
Axes of the slice: x: 2, y: 2, z: 4, core: 2. Of those that a mesh axis runs over, the one named last changes fastest.
Arguments:
- small_in: bfloat16 [32, 1024, 768], P('img', 'seq'), may hold values from -6 to 6
- large_in: bfloat16 [32, 640, 768], P('img', 'seq'), may hold values from -6 to 6
- small_cot: bfloat16 [32, 1024, 768], P('img', 'seq'), may hold values from -6 to 6
- large_cot: bfloat16 [32, 640, 768], P('img', 'seq'), may hold values from -6 to 6
- first_gain: float32 [768], replicated, may hold values from 0.5 to 1.5
- first_bias: float32 [768], replicated, may hold values from -1.75 to 1.75
- query_weight: bfloat16 [768, 768], P('img'), may hold values from -0.21875 to 0.21875
- query_bias: float32 [768], replicated, may hold values from -1.75 to 1.75
- key_weight: bfloat16 [768, 768], P('img'), may hold values from -0.21875 to 0.21875
- value_weight: bfloat16 [768, 768], P('img'), may hold values from -0.21875 to 0.21875
- value_bias: float32 [768], replicated, may hold values from -1.75 to 1.75
- out_weight: bfloat16 [768, 768], P('img'), may hold values from -1.75 to 1.75
- out_bias: float32 [768], replicated, may hold values from -1.75 to 1.75
- attend_scale: float32 [768], replicated, may hold values from 0.5 to 1.5
- second_gain: float32 [768], replicated, may hold values from 0.5 to 1.5
- second_bias: float32 [768], replicated, may hold values from -1.75 to 1.75
- up_weight: bfloat16 [768, 3072], P('img'), may hold values from -0.21875 to 0.21875
- up_bias: float32 [3072], replicated, may hold values from -1.75 to 1.75
- down_weight: bfloat16 [3072, 768], P('img'), may hold values from -0.109375 to 0.109375
- down_bias: float32 [768], replicated, may hold values from -1.75 to 1.75
- feed_scale: float32 [768], replicated, may hold values from 0.5 to 1.5
- rel_table: float32 [12, 2212], replicated, may hold values from -6 to 6
Outputs:
- small_out: bfloat16 [32, 1024, 768], P('img', 'seq')
- large_out: bfloat16 [32, 640, 768], P('img', 'seq')
- small_grad: bfloat16 [32, 1024, 768], P('img', 'seq')
- large_grad: bfloat16 [32, 640, 768], P('img', 'seq')
- grad_first_gain: float32 [768], replicated
- grad_first_bias: float32 [768], replicated
- grad_query: float32 [768, 768], P('img')
- grad_query_bias: float32 [768], replicated
- grad_key: float32 [768, 768], P('img')
- grad_value: float32 [768, 768], P('img')
- grad_value_bias: float32 [768], replicated
- grad_out: float32 [768, 768], P('img')
- grad_out_bias: float32 [768], replicated
- grad_attend_scale: float32 [768], replicated
- grad_second_gain: float32 [768], replicated
- grad_second_bias: float32 [768], replicated
- grad_up: float32 [768, 3072], P('img')
- grad_up_bias: float32 [3072], replicated
- grad_down: float32 [3072, 768], P('img')
- grad_down_bias: float32 [768], replicated
- grad_feed_scale: float32 [768], replicated
- grad_rel_table: float32 [12, 2212], replicated
All inputs are finite; a program needn't handle non-finite values.
Results may differ from a plain program's by a relative error of at most 0.015.
Values may be sent and summed in bfloat16 or wider, within the bound.
A program may use at most 448 MiB of HBM per device.

v0:
```python
import jax
import jax.numpy as jnp
from jax import lax
from jax.sharding import PartitionSpec as P

HEADS = 12
SGRID = 14
LGRID = 24
SLEN = 256
LLEN = 640


NEGATIVE = -1e30
EPSILON = 1e-06


def shifted(array, axis, by):
    count = lax.axis_size(axis)
    return lax.ppermute(array, axis, [(i, (i + by) % count) for i in range(count)])


def layer_norm(values, gain, bias):
    center = values - jnp.mean(values, axis=-1, keepdims=True)
    spread = jnp.mean(center * center, axis=-1, keepdims=True)
    return center * lax.rsqrt(spread + EPSILON) * gain + bias


def matmul(left, right):
    return jnp.dot(left, right, preferred_element_type=jnp.float32)


def position_bias(table, places, length, grid):
    heads = table.shape[0]
    span = 2 * LGRID - 1
    total_rel = table.shape[1]
    queries_count = places.shape[0]
    grid_table = table[:, : span * span].reshape(heads, span, span)
    patch = places - 1
    query_row = patch // grid
    query_col = patch % grid
    steps_all = jnp.arange(span, dtype=jnp.int32)
    cells = jnp.arange(grid, dtype=jnp.int32)
    row_hot = (
        steps_all[None, :, None] == query_row[:, None, None] - cells[None, None, :] + LGRID - 1
    ).astype(jnp.float32)
    col_hot = (
        steps_all[None, :, None] == query_col[:, None, None] - cells[None, None, :] + LGRID - 1
    ).astype(jnp.float32)
    partial_bias = jnp.einsum("hab,qbc->hqac", grid_table, col_hot, precision=lax.Precision.HIGHEST)
    patches = jnp.einsum(
        "qar,hqac->hqrc", row_hot, partial_bias, precision=lax.Precision.HIGHEST
    ).reshape(heads, queries_count, grid * grid)
    rest = length - 1 - grid * grid
    class_key = jnp.broadcast_to(table[:, total_rel - 2][:, None, None], (heads, queries_count, 1))
    patch_rows = jnp.concatenate(
        [class_key, patches, jnp.zeros((heads, queries_count, rest), jnp.float32)], axis=2
    )
    class_row = jnp.concatenate(
        [
            table[:, total_rel - 1][:, None],
            jnp.broadcast_to(table[:, total_rel - 3][:, None], (heads, grid * grid)),
            jnp.zeros((heads, rest), jnp.float32),
        ],
        axis=1,
    )
    is_class = (places == 0)[None, :, None]
    return jnp.where(is_class, class_row[:, None, :], patch_rows)


def to_heads(block, heads):
    groups, rows, width = block.shape
    return block.reshape(groups, rows, heads, width // heads)


def block_scores(query, key, query_rows, key_rows, length, bias_full):
    size = query.shape[-1] // HEADS
    raw = jnp.einsum(
        "gqhd,gkhd->ghqk",
        to_heads(query, HEADS),
        to_heads(key, HEADS),
        preferred_element_type=jnp.float32,
    )
    key_place = key_rows % length
    select = (key_place[:, None] == jnp.arange(length, dtype=jnp.int32)[None, :]).astype(
        jnp.float32
    )
    bias_block = jnp.einsum("hql,kl->hqk", bias_full, select, precision=lax.Precision.HIGHEST)
    allowed = (query_rows // length)[:, None] == (key_rows // length)[None, :]
    scores = raw * float(size) ** (-0.5) + bias_block[None]
    return (scores, allowed, select)


def key_rows_of(source, count_keys):
    return source * count_keys + jnp.arange(count_keys, dtype=jnp.int32)


def allowed_mask(allowed, key_rows, length, grid):
    return allowed & (key_rows % length < grid * grid + 1)[None, :]


def absorb_one(state, query, key, value, query_rows, key_rows, info):
    length, grid, bias_full = info
    maximum, total, accum = state
    scores, allowed, select = block_scores(query, key, query_rows, key_rows, length, bias_full)
    allowed = allowed_mask(allowed, key_rows, length, grid)
    masked = jnp.where(allowed[None, None], scores, NEGATIVE)
    newmax = jnp.maximum(maximum, jnp.max(masked, axis=-1))
    weights = jnp.where(allowed[None, None], jnp.exp(scores - newmax[..., None]), 0.0)
    factor = jnp.exp(maximum - newmax)
    total = total * factor + jnp.sum(weights, axis=-1)
    accum = accum * factor[..., None] + jnp.einsum(
        "ghqk,gkhd->ghqd",
        weights.astype(jnp.bfloat16),
        to_heads(value, HEADS),
        preferred_element_type=jnp.float32,
    )
    return (newmax, total, accum)


def absorb_cycle(states, queries, moving, members, query_rows, source, info):
    states = list(states)
    for which, offset, rows in members:
        key = moving[0][:, offset : offset + rows]
        value = moving[1][:, offset : offset + rows]
        states[which] = absorb_one(
            states[which],
            queries[which],
            key,
            value,
            query_rows[which],
            key_rows_of(source, rows),
            info[which],
        )
    return tuple(states)


def pass_forward(moving):
    return shifted((moving[0], moving[1]), "seq", 1)


def cycle_forward(queries, cycle_pair, members, query_rows, info):
    position = lax.axis_index("seq")
    count = lax.axis_size("seq")
    states = []
    for which in range(2):
        groups, rows, width = queries[which].shape
        states.append(
            (
                jnp.full((groups, HEADS, rows), NEGATIVE, jnp.float32),
                jnp.zeros((groups, HEADS, rows), jnp.float32),
                jnp.zeros((groups, HEADS, rows, width // HEADS), jnp.float32),
            )
        )
    states = absorb_cycle(tuple(states), queries, cycle_pair, members, query_rows, position, info)

    def turn(step, carry):
        held_states, moving = carry
        moving = tuple(pass_forward(moving))
        held_states = absorb_cycle(
            held_states, queries, moving, members, query_rows, (position - step) % count, info
        )
        return (held_states, moving)

    states, moving = lax.fori_loop(1, count, turn, (states, cycle_pair))
    attended = []
    logsums = []
    for which in range(2):
        maximum, total, accum = states[which]
        groups, heads_count, rows, size = accum.shape
        attended.append(
            jnp.transpose(accum / total[..., None], (0, 2, 1, 3)).reshape(
                groups, rows, heads_count * size
            )
        )
        logsums.append(maximum + jnp.log(total))
    return (tuple(attended), tuple(logsums))


def visit_one(query, dout, logsum, delta, key, value, query_rows, key_rows, info):
    length, grid, bias_full = info
    groups, count_keys, width = key.shape
    scale = float(width // HEADS) ** (-0.5)
    scores, allowed, select = block_scores(query, key, query_rows, key_rows, length, bias_full)
    allowed = allowed_mask(allowed, key_rows, length, grid)
    probs = jnp.where(allowed[None, None], jnp.exp(scores - logsum[..., None]), 0.0)
    dout_heads = to_heads(dout, HEADS)
    dprobs = jnp.einsum(
        "gqhd,gkhd->ghqk", dout_heads, to_heads(value, HEADS), preferred_element_type=jnp.float32
    )
    dscores = (probs * (dprobs - delta[..., None])).astype(jnp.bfloat16)
    dq_term = scale * jnp.einsum(
        "ghqk,gkhd->gqhd", dscores, to_heads(key, HEADS), preferred_element_type=jnp.float32
    )
    dkey_term = jnp.einsum(
        "ghqk,gqhd->gkhd", dscores, to_heads(query, HEADS), preferred_element_type=jnp.float32
    )
    dvalue_term = jnp.einsum(
        "ghqk,gqhd->gkhd",
        probs.astype(jnp.bfloat16),
        dout_heads,
        preferred_element_type=jnp.float32,
    )
    summed = jnp.sum(dscores.astype(jnp.float32), axis=0)
    bias_term = jnp.einsum("hqk,kl->hql", summed, select, precision=lax.Precision.HIGHEST)
    return (
        dq_term,
        scale * dkey_term.reshape(groups, count_keys, width),
        dvalue_term.reshape(groups, count_keys, width),
        bias_term,
    )


def visit_cycle(carry, queries, douts, logsums, deltas, moving, members, query_rows, source, info):
    dqueries, dpair, bias_grads = carry
    dqueries = list(dqueries)
    bias_grads = list(bias_grads)
    key_pieces = []
    value_pieces = []
    for which, offset, rows in members:
        key = moving[0][:, offset : offset + rows]
        value = moving[1][:, offset : offset + rows]
        dq_term, dk_term, dv_term, bias_term = visit_one(
            queries[which],
            douts[which],
            logsums[which],
            deltas[which],
            key,
            value,
            query_rows[which],
            key_rows_of(source, rows),
            info[which],
        )
        dqueries[which] = dqueries[which] + dq_term
        key_pieces.append(dk_term)
        value_pieces.append(dv_term)
        bias_grads[which] = bias_grads[which] + bias_term
    new_pair = (
        dpair[0] + jnp.concatenate(key_pieces, axis=1),
        dpair[1] + jnp.concatenate(value_pieces, axis=1),
    )
    return (tuple(dqueries), new_pair, tuple(bias_grads))


def send_grads(dpair):
    return tuple(shifted((dpair[0], dpair[1]), "seq", 1))


def cycle_backward(queries, douts, logsums, deltas, cycle_pair, members, query_rows, info, start):
    position = lax.axis_index("seq")
    count = lax.axis_size("seq")
    dpair = tuple((jnp.zeros(item.shape, jnp.float32) for item in cycle_pair))

    def turn(step, state):
        carry, moving = state
        carry = visit_cycle(
            carry,
            queries,
            douts,
            logsums,
            deltas,
            moving,
            members,
            query_rows,
            (position - step) % count,
            info,
        )
        moving = tuple(shifted((moving[0], moving[1]), "seq", 1))
        return ((carry[0], send_grads(carry[1]), carry[2]), moving)

    carry, moving = lax.fori_loop(0, count - 1, turn, ((start[0], dpair, start[1]), cycle_pair))
    carry = visit_cycle(
        carry,
        queries,
        douts,
        logsums,
        deltas,
        moving,
        members,
        query_rows,
        (position - count + 1) % count,
        info,
    )
    return (carry[0], send_grads(carry[1]), carry[2])


def per_device(
    small_in,
    large_in,
    small_cot,
    large_cot,
    first_gain,
    first_bias,
    query_weight,
    query_bias,
    key_weight,
    value_weight,
    value_bias,
    out_weight,
    out_bias,
    attend_scale,
    second_gain,
    second_bias,
    up_weight,
    up_bias,
    down_weight,
    down_bias,
    feed_scale,
    rel_table,
):
    groups, small_rows, width = small_in.shape
    large_rows = large_in.shape[1]
    all_rows = small_rows + large_rows
    position = lax.axis_index("seq")
    query_rows = (
        position * small_rows + jnp.arange(small_rows, dtype=jnp.int32),
        position * large_rows + jnp.arange(large_rows, dtype=jnp.int32),
    )
    small_places = query_rows[0] % SLEN
    large_places = query_rows[1] % LLEN

    def make_biases(table):
        return (
            position_bias(table, small_places, SLEN, SGRID),
            position_bias(table, large_places, LLEN, LGRID),
        )

    biases, bias_back = jax.vjp(make_biases, rel_table)
    info = ((SLEN, SGRID, biases[0]), (LLEN, LGRID, biases[1]))
    valid_rows = jnp.concatenate(
        [small_places < SGRID * SGRID + 1, large_places < LGRID * LGRID + 1]
    )
    valid_flat = jnp.broadcast_to(valid_rows[None, :], (groups, all_rows)).reshape(-1)
    w_query, w_key, w_value, w_out, w_up, w_down = (
        lax.all_gather(query_weight, "img", axis=0, tiled=True),
        lax.all_gather(key_weight, "img", axis=0, tiled=True),
        lax.all_gather(value_weight, "img", axis=0, tiled=True),
        lax.all_gather(out_weight, "img", axis=0, tiled=True),
        lax.all_gather(up_weight, "img", axis=0, tiled=True),
        lax.all_gather(down_weight, "img", axis=0, tiled=True),
    )

    def split(rows_array):
        shaped = rows_array.reshape(groups, all_rows, -1)
        return (shaped[:, :small_rows], shaped[:, small_rows:])

    inputs = jnp.concatenate([small_in, large_in], axis=1).astype(jnp.float32).reshape(-1, width)
    hidden = layer_norm(inputs, first_gain, first_bias).astype(jnp.bfloat16)
    query = (matmul(hidden, w_query) + query_bias).astype(jnp.bfloat16)
    key = matmul(hidden, w_key).astype(jnp.bfloat16)
    value = (matmul(hidden, w_value) + value_bias).astype(jnp.bfloat16)
    queries = split(query)
    cycle_pair = (key.reshape(groups, all_rows, width), value.reshape(groups, all_rows, width))
    members = ((0, 0, small_rows), (1, small_rows, large_rows))
    attended, logsums = cycle_forward(queries, cycle_pair, members, query_rows, info)
    mixed = (
        jnp.concatenate([attended[0], attended[1]], axis=1).reshape(-1, width).astype(jnp.bfloat16)
    )
    branch = matmul(mixed, w_out) + out_bias
    residual = inputs + attend_scale * branch
    hidden2 = layer_norm(residual, second_gain, second_bias).astype(jnp.bfloat16)
    upper = matmul(hidden2, w_up) + up_bias
    active = jax.nn.gelu(upper, approximate=False).astype(jnp.bfloat16)
    lower = matmul(active, w_down) + down_bias
    output = jnp.where(valid_flat[:, None], residual + feed_scale * lower, 0.0).astype(jnp.bfloat16)
    small_out, large_out = split(output)
    upstream = (
        jnp.concatenate([small_cot, large_cot], axis=1).astype(jnp.float32).reshape(-1, width)
    )
    upstream = upstream * valid_flat[:, None].astype(jnp.float32)
    grad_feed_scale = jnp.sum(upstream * lower, axis=0)
    dlower = (upstream * feed_scale).astype(jnp.bfloat16)
    grad_down_bias = jnp.sum(dlower.astype(jnp.float32), axis=0)
    grad_down = jnp.einsum("rf,rd->fd", active, dlower, preferred_element_type=jnp.float32)
    dactive = jnp.einsum("rd,fd->rf", dlower, w_down, preferred_element_type=jnp.float32)
    unused, gelu_back = jax.vjp(lambda inner: jax.nn.gelu(inner, approximate=False), upper)
    dupper = gelu_back(dactive)[0].astype(jnp.bfloat16)
    grad_up_bias = jnp.sum(dupper.astype(jnp.float32), axis=0)
    grad_up = jnp.einsum("rd,rf->df", hidden2, dupper, preferred_element_type=jnp.float32)
    dhidden2 = jnp.einsum("rf,df->rd", dupper, w_up, preferred_element_type=jnp.float32)
    unused, second_back = jax.vjp(layer_norm, residual, second_gain, second_bias)
    dres_part, grad_second_gain, grad_second_bias = second_back(dhidden2)
    dresidual = upstream + dres_part
    grad_attend_scale = jnp.sum(dresidual * branch, axis=0)
    dbranch = (dresidual * attend_scale).astype(jnp.bfloat16)
    grad_out_bias = jnp.sum(dbranch.astype(jnp.float32), axis=0)
    grad_out = jnp.einsum("rd,re->de", mixed, dbranch, preferred_element_type=jnp.float32)
    dmixed = jnp.einsum("re,de->rd", dbranch, w_out, preferred_element_type=jnp.float32).astype(
        jnp.bfloat16
    )
    held, held_sums = cycle_forward(queries, cycle_pair, members, query_rows, info)
    douts = split(dmixed)
    deltas = tuple(
        (
            jnp.einsum(
                "gqhd,gqhd->ghq",
                to_heads(douts[which].astype(jnp.float32), HEADS),
                to_heads(held[which], HEADS),
            )
            for which in range(2)
        )
    )
    dq_start = tuple(
        (jnp.zeros(to_heads(queries[which], HEADS).shape, jnp.float32) for which in range(2))
    )
    bias_start = tuple((jnp.zeros(item.shape, jnp.float32) for item in biases))
    dqueries, dpair, bias_grads = cycle_backward(
        queries,
        douts,
        held_sums,
        deltas,
        cycle_pair,
        members,
        query_rows,
        info,
        (dq_start, bias_start),
    )
    table_grad = bias_back(bias_grads)[0]
    dquery = jnp.concatenate(
        [
            dqueries[0].reshape(groups, small_rows, width),
            dqueries[1].reshape(groups, large_rows, width),
        ],
        axis=1,
    )
    dquery = dquery.reshape(-1, width).astype(jnp.bfloat16)
    dkey = dpair[0].reshape(-1, width).astype(jnp.bfloat16)
    dvalue = dpair[1].reshape(-1, width).astype(jnp.bfloat16)
    grad_query_bias = jnp.sum(dquery.astype(jnp.float32), axis=0)
    grad_value_bias = jnp.sum(dvalue.astype(jnp.float32), axis=0)
    grad_query = jnp.einsum("rd,re->de", hidden, dquery, preferred_element_type=jnp.float32)
    grad_key = jnp.einsum("rd,re->de", hidden, dkey, preferred_element_type=jnp.float32)
    grad_value = jnp.einsum("rd,re->de", hidden, dvalue, preferred_element_type=jnp.float32)
    dhidden = (
        jnp.einsum("re,de->rd", dquery, w_query, preferred_element_type=jnp.float32)
        + jnp.einsum("re,de->rd", dkey, w_key, preferred_element_type=jnp.float32)
        + jnp.einsum("re,de->rd", dvalue, w_value, preferred_element_type=jnp.float32)
    )
    unused, first_back = jax.vjp(layer_norm, inputs, first_gain, first_bias)
    dinput_part, grad_first_gain, grad_first_bias = first_back(dhidden)
    dinputs = (dresidual + dinput_part).astype(jnp.bfloat16)
    small_grad, large_grad = split(dinputs)
    shares = (
        lax.psum_scatter(grad_query, "img", scatter_dimension=0, tiled=True),
        lax.psum_scatter(grad_key, "img", scatter_dimension=0, tiled=True),
        lax.psum_scatter(grad_value, "img", scatter_dimension=0, tiled=True),
        lax.psum_scatter(grad_out, "img", scatter_dimension=0, tiled=True),
        lax.psum_scatter(grad_up, "img", scatter_dimension=0, tiled=True),
        lax.psum_scatter(grad_down, "img", scatter_dimension=0, tiled=True),
    )
    shares = lax.psum((shares[0], shares[1], shares[2], shares[3], shares[4], shares[5]), "seq")
    smalls = lax.psum(
        (
            grad_first_gain,
            grad_first_bias,
            grad_query_bias,
            grad_value_bias,
            grad_out_bias,
            grad_attend_scale,
            grad_second_gain,
            grad_second_bias,
            grad_up_bias,
            grad_down_bias,
            grad_feed_scale,
            table_grad,
        ),
        ("img", "seq"),
    )
    return (
        small_out,
        large_out,
        small_grad,
        large_grad,
        smalls[0],
        smalls[1],
        shares[0],
        smalls[2],
        shares[1],
        shares[2],
        smalls[3],
        shares[3],
        smalls[4],
        smalls[5],
        smalls[6],
        smalls[7],
        shares[4],
        smalls[8],
        shares[5],
        smalls[9],
        smalls[10],
        smalls[11],
    )


def solution(mesh):
    return jax.shard_map(
        per_device,
        mesh=mesh,
        in_specs=(
            P("img", "seq", None),
            P("img", "seq", None),
            P("img", "seq", None),
            P("img", "seq", None),
            P(),
            P(),
            P("img", None),
            P(),
            P("img", None),
            P("img", None),
            P(),
            P("img", None),
            P(),
            P(),
            P(),
            P(),
            P("img", None),
            P(),
            P("img", None),
            P(),
            P(),
            P(),
        ),
        out_specs=(
            P("img", "seq", None),
            P("img", "seq", None),
            P("img", "seq", None),
            P("img", "seq", None),
            P(),
            P(),
            P("img", None),
            P(),
            P("img", None),
            P("img", None),
            P(),
            P("img", None),
            P(),
            P(),
            P(),
            P(),
            P("img", None),
            P(),
            P("img", None),
            P(),
            P(),
            P(),
        ),
        check_vma=False,
    )
```

profile of v0, /device:TPU:0, one launch (start us, length us, event | category | flops | bytes accessed | tf_op | source)
XLA Modules:
  0.0 1866.7 jit_solution(1256923358427059439)
XLA Ops:
  24.4 12.0 convolution_bitcast_fusion.2
  36.4 46.9 %copy.184 = f32[12,320,47,24]{2,3,0,1:T(8,128)} copy(f32[12,320,47,24]{1,2,0,3:T(8,128)} %convolution_bitcast_fusion.2) | data formatting | bytes 34652160 | tf_op jit(solution)/shard_map/jvp(hab,qbc->hqac)/transpose | solution.py:49
  83.4 42.4 %convolution_bitcast_fusion = f32[12,320,24,24]{2,3,0,1:T(8,128)} fusion(f32[12,320,47,24]{2,3,0,1:T(8,128)} %copy.184, s32[320,24]{1,0:T(8,128)S(1)} %copy.183), kind=kOutput, calls=%fused_computation.45 | convolution fusion | flops 1247838720 | bytes 26204160 | tf_op jit(solution)/shard_map/jvp(qar,hqac->hqrc)/dot_general | solution.py:50
  125.8 40.2 %copy.185 = f32[12,320,24,24]{1,3,2,0:T(8,128)} copy(f32[12,320,24,24]{2,3,0,1:T(8,128)} %convolution_bitcast_fusion) | data formatting | bytes 17694720 | tf_op jit(solution)/shard_map/jvp(qar,hqac->hqrc)/transpose | solution.py:50
  166.0 12.5 copy.186
  179.7 14.4 fusion.129
  194.1 10.5 fusion.124
  204.6 11.1 convolution_bitcast_fusion.3
  215.7 41.5 %copy.169 = f32[12,512,47,14]{2,3,0,1:T(8,128)} copy(f32[12,512,47,14]{1,2,0,3:T(8,128)} %convolution_bitcast_fusion.3) | data formatting | bytes 32342016 | tf_op jit(solution)/shard_map/jvp(hab,qbc->hqac)/transpose | solution.py:49
  257.4 42.6 %convolution_bitcast_fusion.1 = f32[12,512,14,14]{2,3,0,1:T(8,128)} fusion(f32[12,512,47,14]{2,3,0,1:T(8,128)} %copy.169, s32[512,14]{1,0:T(8,128)S(1)} %copy.168), kind=kOutput, calls=%fused_computation.46 | convolution fusion | flops 679519232 | bytes 21016576 | tf_op jit(solution)/shard_map/jvp(qar,hqac->hqrc)/dot_general | solution.py:50
  300.0 31.0 %copy.170 = f32[12,512,14,14]{1,3,2,0:T(8,128)} copy(f32[12,512,14,14]{2,3,0,1:T(8,128)} %convolution_bitcast_fusion.1) | data formatting | bytes 9633792 | tf_op jit(solution)/shard_map/jvp(qar,hqac->hqrc)/transpose | solution.py:50
  336.8 11.7 fusion.75
  348.5 10.5 fusion.76
  359.8 13.1 fusion.134
  372.9 9.6 fusion.74
  434.7 10.4 select_reduce_fusion.3
  445.1 14.8 select_reduce_fusion.1
  478.9 8.5 fusion.41
  487.5 14.1 select_reduce_fusion
  501.7 15.7 fusion.8
  518.1 11.6 fusion.17
  536.5 9.6 fusion.46
  546.2 9.3 fusion.226
  562.4 17.0 fusion.28
  579.4 18.0 fusion.227
  603.7 6.9 fusion.225
  614.3 57.6 %multiply_convert_fusion.2 = (bf16[1664,3072]{1,0:T(8,128)(2,1)}, f32[1664,3072]{1,0:T(8,128)}, f32[1664,3072]{1,0:T(8,128)}) fusion(f32[3072]{0:T(1024)S(1)} %copy-done.165, bf16[768,3072]{1,0:T(8,128)(2,1)} %all-gather.15.cloned.1.call-done, f32[1664,768]{1,0:T(8,128)} %copy-done.54, f32[768]{0:T(1024)S(1)} %copy-done.170, f32[768]{0:T(1024)S(1)} %copy-done.168, ...), kind=kOutput, calls=%fused_computation.26 | convolution fusion | flops 8195506176 | bytes 60980224 | tf_op jit(solution)/shard_map/dot_general | solution.py:29
  671.9 28.5 %convert_reduce_fusion.2 = (f32[3072]{0:T(1024)}, bf16[1664,3072]{1,0:T(8,128)(2,1)}) fusion(f32[1664,3072]{1,0:T(8,128)} %get-tuple-element.255, bf16[1664,768]{1,0:T(8,128)(2,1)} %multiply_convert_fusion.7, bf16[3072,768]{1,0:T(8,128)(2,1)} %all-gather.17.cloned.1.call-done, f32[1664,3072]{1,0:T(8,128)} %get-tuple-element.298, f32[3072]{0:T(1024)S(1)} %copy-done.165), kind=kOutput, calls=%fused_computation.24 | convolution fusion | flops 7938634752 | bytes 58417152 | tf_op jit(solution)/shard_map/rd,fd->rf/dot_general | solution.py:374
  700.5 16.1 multiply_reduce_fusion.1
  716.7 17.9 fusion.223
  744.3 10.4 fusion.44
  754.7 13.1 convert_reduce_fusion.4
  767.8 13.2 convert_reduce_fusion.3
  794.0 26.3 %convert_reduce_fusion = (f32[12,512,512]{1,2,0:T(8,128)}, bf16[2,12,512,512]{2,3,1,0:T(8,128)(2,1)}) fusion(f32[2,12,512]{2,1,0:T(8,128)S(1)} %fusion.83, bf16[2,512,12,64]{1,3,2,0:T(8,128)(2,1)S(1)} %bitcast.367, bf16[2,512,12,64]{1,3,2,0:T(8,128)(2,1)} %bitcast.397, f32[2,12,512]{2,1,0:T(8,128)S(1)} %copy-done.67, f32[12,512,512]{1,2,0:T(8,128)} %fusion.75, ...), kind=kOutput, calls=%fused_computation.9 | convolution fusion | flops 858783744 | bytes 66420736 | tf_op jit(solution)/shard_map/gqhd,gkhd->ghqk/dot_general | solution.py:187
  820.3 24.9 %convert_reduce_fusion.1 = (f32[12,512,512]{1,2,0:T(8,128)}, bf16[2,12,512,512]{2,3,1,0:T(8,128)(2,1)}) fusion(f32[2,12,512]{2,1,0:T(8,128)S(1)} %fusion.83, bf16[2,512,12,64]{1,3,2,0:T(8,128)(2,1)S(1)} %bitcast.368, bf16[2,512,12,64]{1,3,2,0:T(8,128)(2,1)S(1)} %bitcast.395, f32[2,12,512]{2,1,0:T(8,128)S(1)} %copy-done.67, f32[12,512,512]{1,2,0:T(8,128)} %fusion.74, ...), kind=kOutput, calls=%fused_computation.10 | convolution fusion | flops 858783744 | bytes 66420736 | tf_op jit(solution)/shard_map/while/body/eval_jaxpr/gqhd,gkhd->ghqk/dot_general | solution.py:187
  845.3 9.2 fusion.228
  854.4 7.0 convolution_multiply_fusion.1
  869.9 8.4 add_multiply_fusion
  898.3 6.4 convolution_bitcast_fusion.6
  904.8 17.3 fusion.26
  931.0 10.6 convolution_multiply_fusion
  958.4 45.7 %collective-permute-done.2 = f32[2,832,768]{2,1,0:T(8,128)} collective-permute-done((f32[2,832,768]{2,1,0:T(8,128)}, f32[2,832,768]{2,1,0:T(8,128)}, u32[]{:S(2)}, u32[]{:S(2)}) %collective-permute-start.2) | collective-permute-done | bytes 5111840 | tf_op jit(solution)/shard_map/while/body/eval_jaxpr/ppermute | solution.py:19
  1012.1 10.4 fusion.48
  1025.4 16.4 fusion.30
  1045.4 121.7 %collective-permute-done.3 = bf16[2,832,768]{2,1,0:T(8,128)(2,1)} collective-permute-done((bf16[2,832,768]{2,1,0:T(8,128)(2,1)}, bf16[2,832,768]{2,1,0:T(8,128)(2,1)}, u32[]{:S(2)}, u32[]{:S(2)}) %collective-permute-start.3) | collective-permute-done | bytes 2555936 | tf_op jit(solution)/shard_map/ppermute | solution.py:19
  1179.7 54.4 %collective-permute-done.5 = bf16[2,832,768]{2,1,0:T(8,128)(2,1)S(1)} collective-permute-done((bf16[2,832,768]{2,1,0:T(8,128)(2,1)S(1)}, bf16[2,832,768]{2,1,0:T(8,128)(2,1)S(1)}, u32[]{:S(2)}, u32[]{:S(2)}) %collective-permute-start.5) | collective-permute-done | bytes 2555936 | tf_op jit(solution)/shard_map/ppermute | solution.py:19
  1240.0 16.0 fusion.220
  1259.1 14.5 fusion.233
  1274.3 12.5 fusion.141
  1289.1 12.2 select_reduce_fusion.5
  1312.2 39.7 %copy.239 = f32[12,512,14,14]{2,3,0,1:T(8,128)} copy(f32[12,512,14,14]{1,3,2,0:T(8,128)} %reshape.1394) | data formatting | bytes 9633792 | tf_op jit(solution)/shard_map/transpose(jvp())/reshape | solution.py:52
  1351.9 53.3 %fusion.23 = f32[512,14,12,47]{3,1,2,0:T(8,128)} fusion(f32[12,512,14,14]{2,3,0,1:T(8,128)} %copy.239, s32[512,14]{1,0:T(8,128)S(1)} %copy-done.61), kind=kOutput, calls=%fused_computation.44 | convolution fusion | flops 679519232 | bytes 21016576 | tf_op jit(solution)/shard_map/transpose(jvp(qar,hqac->hqrc))/dot_general | solution.py:50
  1405.3 51.4 %fusion.111 = f32[12,47,47]{2,1,0:T(8,128)S(1)} fusion(f32[512,14,12,47]{3,1,2,0:T(8,128)} %fusion.23, s32[512,14]{0,1:T(8,128)S(1)} %copy-done.89), kind=kOutput, calls=%fused_computation.187 | convolution fusion | flops 2280449024 | bytes 16305712 | tf_op jit(solution)/shard_map/transpose(jvp(hab,qbc->hqac))/dot_general | solution.py:49
  1458.4 13.7 fusion.127
  1472.1 15.1 select_reduce_fusion.4
  1490.8 6.3 split.35
  1497.0 11.7 copy.232
  1508.8 43.1 %copy.233 = f32[12,320,24,24]{2,3,0,1:T(8,128)} copy(f32[12,320,24,24]{1,3,2,0:T(8,128)} %bitcast.381) | data formatting | bytes 17694720 | tf_op jit(solution)/shard_map/transpose(jvp())/reshape | solution.py:52
  1551.9 42.2 %fusion.20 = f32[320,24,12,47]{3,1,2,0:T(8,128)} fusion(f32[12,320,24,24]{2,3,0,1:T(8,128)} %copy.233, s32[320,24]{1,0:T(8,128)S(1)} %copy-done.63), kind=kOutput, calls=%fused_computation.43 | convolution fusion | flops 1247838720 | bytes 26204160 | tf_op jit(solution)/shard_map/transpose(jvp(qar,hqac->hqrc))/dot_general | solution.py:50
  1594.1 67.7 %fusion.116 = f32[12,47,47]{2,1,0:T(8,128)S(1)} fusion(f32[320,24,12,47]{3,1,2,0:T(8,128)} %fusion.20, s32[320,24]{0,1:T(8,128)S(1)} %copy-done.74), kind=kOutput, calls=%fused_computation.188 | convolution fusion | flops 2443338240 | bytes 17462832 | tf_op jit(solution)/shard_map/transpose(jvp(hab,qbc->hqac))/dot_general | solution.py:49
  1682.7 10.3 multiply_reduce_fusion
  1695.9 42.1 %all-reduce.8 = (f32[768]{0:T(1024)}, f32[768]{0:T(1024)}, f32[768]{0:T(1024)}, f32[768]{0:T(1024)}, f32[768]{0:T(1024)}, /*index=5*/f32[768]{0:T(1024)}, f32[76...) all-reduce(f32[768]{0:T(1024)S(1)} %copy-done.122, ...), channel_id=1, replica_groups=mesh['img'=16,'seq'=2] {'img','seq'}, use_global_device_ids=true, to_apply=%region_17.18 | all-reduce | flops 10752 | bytes 86016 | tf_op jit(solution)/shard_map/psum | solution.py:451
  1738.0 48.8 %all-reduce.13.cloned.1.call-done = f32[12,2212]{1,0:T(8,128)} async-done(((f32[12,2212]{1,0:T(8,128)}), f32[12,2212]{1,0:T(8,128)}) %all-reduce.13.cloned.1.call-update) | async-done | bytes 106192 | tf_op jit(solution)/shard_map/psum | solution.py:451
  1786.9 61.2 %all-reduce.15.cloned.1.call-done = (f32[48,768]{1,0:T(8,128)}, f32[48,768]{1,0:T(8,128)}, f32[48,768]{1,0:T(8,128)}, f32[48,768]{1,0:T(8,128)}, f32[48,3072]{1,0:T(8,128)}, /*index=5*/f32[192,768]{1,0:T(8,128)}) async-done(((f32[48,768]{1,0:T(8,128)}, f32[48,768]{1,0:T(8,128)}, f32[48,768]{1,0:T(8,128)}, f32[48,768]{1,0:T(8,128)}, f32[48,3072]{1,0:T(8,128)}, /*index=5*/f32[192,768]{1,0:T(8,128)}), ...) | async-done | bytes 1769488 | tf_op jit(solution)/shard_map/psum | solution.py:450
  (587 shorter events, 287.0 us)
Async XLA Ops:
  7.2 382.6 %all-gather.9.cloned.1.call-start = ((), (), s32[]{:S(2)}) async-start(), calls=%async_computation.7 | async-start | bytes 1253376 | tf_op jit(solution)/shard_map/all_gather | solution.py:335
  7.9 390.7 %all-gather.7.cloned.1.call-start = ((), (), s32[]{:S(2)}) async-start(), calls=%async_computation.6 | async-start | bytes 1253376 | tf_op jit(solution)/shard_map/all_gather | solution.py:334
  8.7 395.7 %all-gather.11.cloned.1.call-start = ((), (), s32[]{:S(2)}) async-start(), calls=%async_computation.8 | async-start | bytes 1253376 | tf_op jit(solution)/shard_map/all_gather | solution.py:336
  9.4 594.2 %all-gather.13.cloned.1.call-start = ((), (), s32[]{:S(2)}) async-start(), calls=%async_computation.9 | async-start | bytes 1253376 | tf_op jit(solution)/shard_map/all_gather | solution.py:337
  10.0 604.3 %all-gather.15.cloned.1.call-start = ((), (), s32[]{:S(2)}) async-start(), calls=%async_computation.10 | async-start | bytes 5013504 | tf_op jit(solution)/shard_map/all_gather | solution.py:338
  10.6 661.3 %all-gather.17.cloned.1.call-start = ((), (), s32[]{:S(2)}) async-start(), calls=%async_computation.11 | async-start | bytes 5013504 | tf_op jit(solution)/shard_map/all_gather | solution.py:339
  11.2 1670.8 %reduce-scatter.7.cloned.1.call-start = ((), (), s32[]{:S(2)}) async-start(), calls=%async_computation.12 | async-start | bytes 2506752 | tf_op jit(solution)/shard_map/reduce_scatter | solution.py:443
  11.3 348.4 %copy-start.161 = (pred[320]{0:T(512)(128)(4,1)}, pred[320]{0:T(512)(128)(4,1)S(1)}, u32[]{:S(2)}) copy-start(pred[320]{0:T(512)(128)(4,1)S(1)} %broadcast_compare_fusion.3) | copy-start | bytes 964
  11.9 167.8 %copy-start.133 = (s32[320]{0:T(512)}, s32[320]{0:T(512)S(1)}, u32[]{:S(2)}) copy-start(s32[320]{0:T(512)S(1)} %add_select_fusion.4) | copy-start | bytes 3844
  83.4 42.5 %copy-start.62 = (s32[320,24]{1,0:T(8,128)}, s32[320,24]{1,0:T(8,128)S(1)}, u32[]{:S(2)}) copy-start(s32[320,24]{1,0:T(8,128)S(1)} %copy.183) | copy-start | bytes 92164
  179.2 203.3 %copy-start.96 = (f32[1664]{0:T(1024)}, f32[1664]{0:T(1024)S(1)}, u32[]{:S(2)}) copy-start(f32[1664]{0:T(1024)S(1)} %rsqrt.25) | copy-start | bytes 19972
  257.4 42.6 %copy-start.60 = (s32[512,14]{1,0:T(8,128)}, s32[512,14]{1,0:T(8,128)S(1)}, u32[]{:S(2)}) copy-start(s32[512,14]{1,0:T(8,128)S(1)} %copy.168) | copy-start | bytes 86020
  348.5 24.3 %slice-start.7 = ((s8[4915200]{0:T(1024)(128)(4,1)}), s8[720896]{0:T(1024)(128)(4,1)S(1)}, s32[]{:S(2)}) async-start(s8[4915200]{0:T(1024)(128)(4,1)} %bitcast.364), calls=%async_computation.27 | async-start | bytes 1441792
  359.7 25.5 %copy-start.98 = (f32[1664]{0:T(1024)}, f32[1664]{0:T(1024)S(1)}, u32[]{:S(2)}) copy-start(f32[1664]{0:T(1024)S(1)} %convert_element_type.224) | copy-start | bytes 19972
  388.4 46.3 %copy-start.56 = (pred[320,320]{0,1:T(8,128)(4,1)}, pred[320,320]{0,1:T(8,128)(4,1)S(1)}, u32[]{:S(2)}) copy-start(pred[320,320]{0,1:T(8,128)(4,1)S(1)} %get-tuple-element.282) | copy-start | bytes 307204
  389.8 55.3 %copy-start.49 = (pred[512,512]{0,1:T(8,128)(4,1)}, pred[512,512]{0,1:T(8,128)(4,1)S(1)}, u32[]{:S(2)}) copy-start(pred[512,512]{0,1:T(8,128)(4,1)S(1)} %get-tuple-element.279) | copy-start | bytes 786436
  389.8 189.6 %copy-start.24 = (pred[512,512]{0,1:T(8,128)(4,1)}, pred[512,512]{0,1:T(8,128)(4,1)S(1)}, u32[]{:S(2)}) copy-start(pred[512,512]{0,1:T(8,128)(4,1)S(1)} %get-tuple-element.278) | copy-start | bytes 786436
  395.7 64.3 %collective-permute-start = (bf16[2,832,768]{2,1,0:T(8,128)(2,1)}, bf16[2,832,768]{2,1,0:T(8,128)(2,1)}, u32[]{:S(2)}, u32[]{:S(2)}) collective-permute-start(bf16[2,832,768]{2,1,0:T(8,128)(2,1)} %bitcast.7), channel_id=1, source_target_pairs={{0,1},{1,0},{2,3},{3,2},{4,5},{5,4},{6,7},{7,6},{8,9},{9,8},{10,11... | collective-permute-start | bytes 7667720 | tf_op jit(solution)/shard_map/while/body/eval_jaxpr/ppermute | solution.py:19
  411.4 121.1 %collective-permute-start.1 = (bf16[2,832,768]{2,1,0:T(8,128)(2,1)}, bf16[2,832,768]{2,1,0:T(8,128)(2,1)}, u32[]{:S(2)}, u32[]{:S(2)}) collective-permute-start(bf16[2,832,768]{2,1,0:T(8,128)(2,1)} %bitcast.17), channel_id=1, source_target_pairs={{0,1},{1,0},{2,3},{3,2},{4,5},{5,4},{6,7},{7,6},{8,9},{9,8},{10,11... | collective-permute-start | bytes 7667720 | tf_op jit(solution)/shard_map/while/body/eval_jaxpr/ppermute | solution.py:19
  428.5 58.9 %copy-start.14 = (bf16[2,512,768]{1,2,0:T(8,128)(2,1)}, bf16[2,512,768]{1,2,0:T(8,128)(2,1)S(1)}, u32[]{:S(2)}) copy-start(bf16[2,512,768]{1,2,0:T(8,128)(2,1)S(1)} %copy.166) | copy-start | bytes 4718596
  501.5 28.1 %copy-start.72 = (f32[2,12,512]{2,1,0:T(8,128)}, f32[2,12,512]{2,1,0:T(8,128)S(1)}, u32[]{:S(2)}) copy-start(f32[2,12,512]{2,1,0:T(8,128)S(1)} %get-tuple-element.291) | copy-start | bytes 147460
  501.6 16.5 copy-start.79
  501.6 16.5 slice-start
  501.6 16.4 slice-start.1
  501.6 16.4 slice-start.2
  501.7 16.4 copy-start.50
  562.4 17.1 copy-start.37
  562.4 17.0 copy-start.82
  610.6 106.0 %copy-start.111 = (f32[1664]{0:T(1024)}, f32[1664]{0:T(1024)S(1)}, u32[]{:S(2)}) copy-start(f32[1664]{0:T(1024)S(1)} %broadcast_multiply_fusion) | copy-start | bytes 19972
  614.2 102.4 %copy-start.142 = (f32[1664]{0:T(1024)}, f32[1664]{0:T(1024)S(1)}, u32[]{:S(2)}) copy-start(f32[1664]{0:T(1024)S(1)} %fusion.169) | copy-start | bytes 19972
  671.9 28.5 %copy-start.55 = (f32[1664,768]{1,0:T(8,128)S(1)}, f32[1664,768]{1,0:T(8,128)}, u32[]{:S(2)}) copy-start(f32[1664,768]{1,0:T(8,128)} %copy-done.54) | copy-start | bytes 15335428
  700.4 16.2 copy-start.154
  716.7 18.0 copy-start.27
  716.7 18.0 copy-start.32
  716.7 18.0 copy-start.99
  716.7 18.0 copy-start.148
  743.3 24.5 %copy-start.12 = (bf16[2,320,768]{1,2,0:T(8,128)(2,1)}, bf16[2,320,768]{1,2,0:T(8,128)(2,1)S(1)}, u32[]{:S(2)}) copy-start(bf16[2,320,768]{1,2,0:T(8,128)(2,1)S(1)} %copy.205) | copy-start | bytes 2949124
  790.9 29.4 %copy-start.7 = (bf16[2,512,768]{1,2,0:T(8,128)(2,1)}, bf16[2,512,768]{1,2,0:T(8,128)(2,1)S(1)}, u32[]{:S(2)}) copy-start(bf16[2,512,768]{1,2,0:T(8,128)(2,1)S(1)} %copy.199) | copy-start | bytes 4718596
  794.0 26.3 %copy-start.36 = (bf16[2,512,768]{1,2,0:T(8,128)(2,1)S(1)}, bf16[2,512,768]{1,2,0:T(8,128)(2,1)}, u32[]{:S(2)}) copy-start(bf16[2,512,768]{1,2,0:T(8,128)(2,1)} %copy.173) | copy-start | bytes 4718596
  890.5 113.5 %collective-permute-start.2 = (f32[2,832,768]{2,1,0:T(8,128)}, f32[2,832,768]{2,1,0:T(8,128)}, u32[]{:S(2)}, u32[]{:S(2)}) collective-permute-start(f32[2,832,768]{2,1,0:T(8,128)} %pad_maximum_fusion), channel_id=1, source_target_pairs={{0,1},{1,0},{2,3},{3,2},{4,5},{5,4},{6,7},{7,6},{8,9},{9,8},{10,11... | collective-permute-start | bytes 15335432 | tf_op jit(solution)/shard_map/while/body/eval_jaxpr/ppermute | solution.py:19
  904.7 777.2 %reduce-scatter.13.cloned.1.call-start = ((), (), s32[]{:S(2)}) async-start(), calls=%async_computation.15 | async-start | bytes 2506752 | tf_op jit(solution)/shard_map/reduce_scatter | solution.py:446
  931.0 242.3 %collective-permute-start.4 = (f32[2,832,768]{2,1,0:T(8,128)}, f32[2,832,768]{2,1,0:T(8,128)}, u32[]{:S(2)}, u32[]{:S(2)}) collective-permute-start(f32[2,832,768]{2,1,0:T(8,128)} %pad_maximum_fusion.1), channel_id=1, source_target_pairs={{0,1},{1,0},{2,3},{3,2},{4,5},{5,4},{6,7},{7,6},{8,9},{9,8},{10,11... | collective-permute-start | bytes 15335432 | tf_op jit(solution)/shard_map/while/body/eval_jaxpr/ppermute | solution.py:19
  957.9 54.1 %copy-start.48 = (pred[320,320]{0,1:T(8,128)(4,1)S(1)}, pred[320,320]{0,1:T(8,128)(4,1)}, u32[]{:S(2)}) copy-start(pred[320,320]{0,1:T(8,128)(4,1)} %get-tuple-element.281) | copy-start | bytes 307204
  957.9 724.0 %reduce-scatter.9.cloned.1.call-start = ((), (), s32[]{:S(2)}) async-start(), calls=%async_computation.13 | async-start | bytes 2506752 | tf_op jit(solution)/shard_map/reduce_scatter | solution.py:444
  958.4 53.7 %copy-start.13 = (bf16[2,320,768]{1,2,0:T(8,128)(2,1)S(1)}, bf16[2,320,768]{1,2,0:T(8,128)(2,1)}, u32[]{:S(2)}) copy-start(bf16[2,320,768]{1,2,0:T(8,128)(2,1)} %copy-done.12) | copy-start | bytes 2949124
  958.4 53.7 %copy-start.68 = (f32[2,12,320]{2,1,0:T(8,128)S(1)}, f32[2,12,320]{2,1,0:T(8,128)}, u32[]{:S(2)}) copy-start(f32[2,12,320]{2,1,0:T(8,128)} %log_add_fusion.1) | copy-start | bytes 92164
  1010.0 157.1 %collective-permute-start.3 = (bf16[2,832,768]{2,1,0:T(8,128)(2,1)}, bf16[2,832,768]{2,1,0:T(8,128)(2,1)}, u32[]{:S(2)}, u32[]{:S(2)}) collective-permute-start(bf16[2,832,768]{2,1,0:T(8,128)(2,1)} %maximum_add_fusion), channel_id=1, source_target_pairs={{0,1},{1,0},{2,3},{3,2},{4,5},{5,4},{6,7},{7,6},{8,9},{9,8},{10,11... | collective-permute-start | bytes 7667720 | tf_op jit(solution)/shard_map/ppermute | solution.py:19
  1041.8 125.3 %copy-start.18 = (bf16[2,320,768]{2,1,0:T(8,128)(2,1)S(1)}, bf16[2,320,768]{2,1,0:T(8,128)(2,1)}, u32[]{:S(2)}) copy-start(bf16[2,320,768]{2,1,0:T(8,128)(2,1)} %param.23) | copy-start | bytes 2949124
  1173.1 508.9 %reduce-scatter.11.cloned.1.call-start = ((), (), s32[]{:S(2)}) async-start(), calls=%async_computation.14 | async-start | bytes 2506752 | tf_op jit(solution)/shard_map/reduce_scatter | solution.py:445
  1177.8 62.1 %copy-start.112 = (f32[1664]{0:T(1024)S(1)}, f32[1664]{0:T(1024)}, u32[]{:S(2)}) copy-start(f32[1664]{0:T(1024)} %copy-done.111) | copy-start | bytes 19972
  1177.8 62.1 %copy-start.143 = (f32[1664]{0:T(1024)S(1)}, f32[1664]{0:T(1024)}, u32[]{:S(2)}) copy-start(f32[1664]{0:T(1024)} %copy-done.142) | copy-start | bytes 19972
  1177.8 62.1 %copy-start.169 = (f32[768]{0:T(1024)S(1)}, f32[768]{0:T(1024)}, u32[]{:S(2)}) copy-start(f32[768]{0:T(1024)} %param.36) | copy-start | bytes 9220
  1177.9 62.1 %copy-start.171 = (f32[768]{0:T(1024)S(1)}, f32[768]{0:T(1024)}, u32[]{:S(2)}) copy-start(f32[768]{0:T(1024)} %param.37) | copy-start | bytes 9220
  1177.9 56.2 %collective-permute-start.5 = (bf16[2,832,768]{2,1,0:T(8,128)(2,1)S(1)}, bf16[2,832,768]{2,1,0:T(8,128)(2,1)S(1)}, u32[]{:S(2)}, u32[]{:S(2)}) collective-permute-start(bf16[2,832,768]{2,1,0:T(8,128)(2,1)S(1)} %maximum_add_fusion.1), channel_id=1, source_target_pairs={{0,1},{1,0},{2,3},{3,2},{4,5},{5,4},{6,7},{7,6},{8,9},{9,8},{10,11... | collective-permute-start | bytes 7667720 | tf_op jit(solution)/shard_map/ppermute | solution.py:19
  1239.9 442.1 %reduce-scatter.15.cloned.1.call-start = ((), (), s32[]{:S(2)}) async-start(), calls=%async_computation.16 | async-start | bytes 10027008 | tf_op jit(solution)/shard_map/reduce_scatter | solution.py:447
  1256.1 425.9 %reduce-scatter.17.cloned.1.call-start = ((), (), s32[]{:S(2)}) async-start(), calls=%async_computation.17 | async-start | bytes 10027008 | tf_op jit(solution)/shard_map/reduce_scatter | solution.py:448
  1273.7 513.2 %all-reduce.13.cloned.1.call-start = ((), (), s32[]{:S(2)}) async-start(), calls=%async_computation.18 | async-start | bytes 294912 | tf_op jit(solution)/shard_map/psum | solution.py:451
  1312.2 39.7 %copy-start.61 = (s32[512,14]{1,0:T(8,128)S(1)}, s32[512,14]{1,0:T(8,128)}, u32[]{:S(2)}) copy-start(s32[512,14]{1,0:T(8,128)} %copy-done.60) | copy-start | bytes 86020
  1351.9 53.3 %copy-start.89 = (s32[512,14]{0,1:T(8,128)S(1)}, s32[512,14]{0,1:T(8,128)}, u32[]{:S(2)}) copy-start(s32[512,14]{0,1:T(8,128)} %copy-done.88) | copy-start | bytes 86020
  1405.3 53.1 %copy-start.134 = (s32[320]{0:T(512)S(1)}, s32[320]{0:T(512)}, u32[]{:S(2)}) copy-start(s32[320]{0:T(512)} %copy-done.133) | copy-start | bytes 3844
  1508.8 43.1 %copy-start.63 = (s32[320,24]{1,0:T(8,128)S(1)}, s32[320,24]{1,0:T(8,128)}, u32[]{:S(2)}) copy-start(s32[320,24]{1,0:T(8,128)} %copy-done.62) | copy-start | bytes 92164
  1551.9 42.2 %copy-start.74 = (s32[320,24]{0,1:T(8,128)S(1)}, s32[320,24]{0,1:T(8,128)}, u32[]{:S(2)}) copy-start(s32[320,24]{0,1:T(8,128)} %copy-done.73) | copy-start | bytes 92164
  1594.1 70.9 %copy-start.66 = (bf16[2,832,768]{2,1,0:T(8,128)(2,1)S(1)}, bf16[2,832,768]{2,1,0:T(8,128)(2,1)}, u32[]{:S(2)}) copy-start(bf16[2,832,768]{2,1,0:T(8,128)(2,1)} %get-tuple-element.251) | copy-start | bytes 7667716
  1665.0 183.0 %all-reduce.15.cloned.1.call-start = ((), (), s32[]{:S(2)}) async-start(), calls=%async_computation.19 | async-start | bytes 3538944 | tf_op jit(solution)/shard_map/psum | solution.py:450
  (145 other events, 1075.5 us)
Sparse Core Ops, SparseCore 0:
  10.3 41.0 all-gather.8
  53.7 37.2 all-gather.6
  93.3 37.2 all-gather.10
  132.7 37.2 all-gather.12
  172.2 52.1 all-gather.14
  226.5 51.7 all-gather.16
  904.8 63.2 reduce-scatter.6
  972.4 61.9 reduce-scatter.12
  1173.2 64.3 reduce-scatter.8
  1241.6 62.2 reduce-scatter.10
  1308.1 110.4 reduce-scatter.14
  1423.1 111.1 reduce-scatter.16
  1665.1 121.6 all-reduce.12
  1789.4 58.6 all-reduce.14
where the time goes:
time: 1880 us; the launch traced here: 1870 us
  matrix products  942 us (50%)
  local copies, waits for them, and re-layouts  403 us (21%)
  waiting for transfers between devices  336 us (18%)
  other arithmetic  116 us (6%)
  blocking collectives  42.1 us (2%)
    ppermute x6, waiting for transfers between devices, shifted(): lax.ppermute(array, axis, [(i, (i + by) % count) for i in range(count)])  222 us
    dot_general x4, matrix products, position_bias(): jnp.einsum('qar,hqac->hqrc', row_hot, partial_bias, precision=lax.Precisi...  181 us
    dot_general x4, matrix products, position_bias(): jnp.einsum('hab,qbc->hqac', grid_table, col_hot, precision=lax.Precision....  142 us
    reshape x5, local copies, waits for them, and re-layouts, position_bias(): patches = jnp.einsum('qar,hqac->hqrc', row_hot, partial_bias, precision=l...  106 us
    dot_general x6, matrix products, matmul(): return jnp.dot(left, right, preferred_element_type=jnp.float32)  99.8 us
    transpose x2, local copies, waits for them, and re-layouts, position_bias(): jnp.einsum('hab,qbc->hqac', grid_table, col_hot, precision=lax.Precision....  88.3 us
    dot_general x4, matrix products, visit_one(): jnp.einsum('gqhd,gkhd->ghqk', dout_heads, to_heads(value, HEADS), preferr...  77.5 us
    transpose x2, local copies, waits for them, and re-layouts, position_bias(): jnp.einsum('qar,hqac->hqrc', row_hot, partial_bias, precision=lax.Precisi...  71.2 us
  transfers between devices with their start and end apart: 20, of which 5 were waited for; matrix products, arithmetic and copies ran while one was open for 65% of the time, Pallas kernels for 0%

commit v1 on v0

--- a/solution.py
+++ b/solution.py
@@ -1,6 +1,10 @@
+import functools
+
 import jax
 import jax.numpy as jnp
 from jax import lax
+from jax.experimental import pallas as pl
+from jax.experimental.pallas import tpu as pltpu
 from jax.sharding import PartitionSpec as P
 
 HEADS = 12
@@ -8,10 +12,733 @@
 LGRID = 24
 SLEN = 256
 LLEN = 640
-
+SPAD = 208
+LPAD = 608
+LANES = 128
 
 NEGATIVE = -1e30
 EPSILON = 1e-06
+F32 = jnp.float32
+BF16 = jnp.bfloat16
+VMEM_BYTES = 62 << 20
+
+
+def dot_nn(left, right):
+    return lax.dot_general(left, right, (((1,), (0,)), ((), ())), preferred_element_type=F32)
+
+
+def dot_nt(left, right):
+    return lax.dot_general(left, right, (((1,), (1,)), ((), ())), preferred_element_type=F32)
+
+
+def normalized(values):
+    center = values - jnp.mean(values, axis=-1, keepdims=True)
+    spread = jnp.mean(center * center, axis=-1, keepdims=True)
+    scale = lax.rsqrt(spread + EPSILON)
+    return center * scale, scale
+
+
+def norm_back(grad, normal, scale):
+    return scale * (
+        grad
+        - jnp.mean(grad, axis=-1, keepdims=True)
+        - normal * jnp.mean(grad * normal, axis=-1, keepdims=True)
+    )
+
+
+def row_sum(values):
+    return jnp.sum(values, axis=0, keepdims=True)
+
+
+def iota(shape, axis):
+    return lax.broadcasted_iota(jnp.int32, shape, axis)
+
+
+L_WIDTH = 1280
+S_WIDTH = 512
+
+
+def table_sequences(table):
+    heads = table.shape[0]
+    span = 2 * LGRID - 1
+    cells = table[:, : span * span].reshape(heads, span, span)
+
+    def sequences(part, grid, width):
+        rows = part.shape[1]
+        low = part[:, :, :grid].reshape(heads, rows * grid)
+        high = jnp.pad(part[:, :, grid:], ((0, 0), (0, 0), (0, 1))).reshape(heads, rows * grid)
+        low = jnp.pad(low, ((0, 0), (0, width - rows * grid)))
+        high = jnp.pad(high, ((0, 0), (grid, width - rows * grid - grid)))
+        return jnp.stack([low, high], axis=1)
+
+    off = LGRID - SGRID
+    large = sequences(cells, LGRID, L_WIDTH)
+    small = sequences(cells[:, off : span - off, off : span - off], SGRID, S_WIDTH)
+    edge = jnp.broadcast_to(
+        jnp.pad(table[:, span * span :], ((0, 0), (0, 5)))[:, :, None], (heads, 8, LANES)
+    )
+    return large, small, edge
+
+
+def table_from_sequences(large, small, edge):
+    heads = large.shape[0]
+    span = 2 * LGRID - 1
+
+    def cells(part, grid):
+        rows = 2 * grid - 1
+        low = part[:, 0, : rows * grid].reshape(heads, rows, grid)
+        high = part[:, 1, grid : grid + rows * grid].reshape(heads, rows, grid)
+        return jnp.concatenate([low, high[:, :, : grid - 1]], axis=2)
+
+    off = LGRID - SGRID
+    total = cells(large, LGRID) + jnp.pad(
+        cells(small, SGRID), ((0, 0), (off, off), (off, off))
+    )
+    return jnp.concatenate([total.reshape(heads, span * span), edge], axis=1)
+
+
+def takes_low(rows, width, grid, first):
+    step = iota((rows, width), 1) % grid
+    row = iota((rows, width), 0)
+    low = step >= grid - 1 + first - row
+    if first == 1:
+        low = low | (row == 0)
+    return low
+
+
+def spread_sequences(seq, rows, width, grid, first):
+    low = jnp.broadcast_to(seq[0:1, :], (rows, width))
+    high = jnp.broadcast_to(seq[1:2, :], (rows, width))
+    chosen = jnp.where(takes_low(rows, width, grid, first), low, high)
+    return pltpu.roll(chosen, 1, 1, stride=1, stride_axis=0)
+
+
+def gather_sequences(spread, rows, width, grid, first):
+    row = iota((rows, width), 0) + 1
+    for bit in (1, 2, 4, 8, 16):
+        spread = jnp.where((row & bit) != 0, pltpu.roll(spread, width - bit, 1), spread)
+    low = takes_low(rows, width, grid, first)
+    return (
+        row_sum(jnp.where(low, spread, 0.0)),
+        row_sum(jnp.where(low, 0.0, spread)),
+    )
+
+
+def large_window(block):
+    start = (LGRID - block) * LGRID
+    return start // LANES, start % LANES
+
+
+def small_window(block):
+    start = (SGRID - 1 - block) * SGRID + SGRID - 1
+    return start // LANES, start % LANES
+
+
+def head_masks():
+    lane = iota((1, LANES), 1)
+    return (
+        jnp.where(lane < LANES // 2, 1.0, 0.0).astype(BF16),
+        jnp.where(lane < LANES // 2, 0.0, 1.0).astype(BF16),
+    )
+
+
+def transposed_biases(large_seq, small_seq, edge, wide, narrow, bias_large, bias_small):
+    patch_q = edge[0:1, 0:1]
+    patch_k = edge[1:2, 0:1]
+    both = edge[2:3, 0:1]
+    wide[...] = spread_sequences(large_seq, 24, L_WIDTH, LGRID, 1)
+    lane = iota((24, LANES), 1)
+    row = iota((24, LANES), 0)
+    for block in range(LGRID + 1):
+        at, turn = large_window(block)
+        piece = wide[:, at * LANES : at * LANES + 768]
+        if turn:
+            piece = pltpu.roll(piece, 768 - turn, 1)
+        piece = piece[:, :640]
+        if block == 0:
+            rest = jnp.where(iota((24, 640), 0) == 0, patch_k, piece)
+        elif block == LGRID:
+            rest = jnp.where(iota((24, 640), 0) == 0, piece, NEGATIVE)
+        else:
+            rest = piece
+        first = jnp.where(lane == 0, patch_q, rest[:, :LANES])
+        if block == 0:
+            first = jnp.where((lane == 0) & (row == 0), both, first)
+        if block == LGRID:
+            first = jnp.where(row == 0, first, NEGATIVE)
+        bias_large[pl.ds(block * 24, 24), 0:LANES] = first
+        bias_large[pl.ds(block * 24, 24), LANES:640] = rest[:, LANES:]
+    bias_large[pl.ds(600, 8), :] = jnp.full((8, 640), NEGATIVE, F32)
+    narrow[...] = spread_sequences(small_seq, 16, S_WIDTH, SGRID, 0)
+    for block in range(SGRID):
+        at, turn = small_window(block)
+        piece = narrow[:, at * LANES : at * LANES + 384]
+        if turn:
+            piece = pltpu.roll(piece, 384 - turn, 1)
+        bias_small[pl.ds(1 + SGRID * block, SGRID), :] = piece[:SGRID, :256]
+    whole = bias_small[...]
+    lane = iota((SPAD, 256), 1)
+    row = iota((SPAD, 256), 0)
+    whole = jnp.where(lane == 0, patch_q, whole)
+    whole = jnp.where(row == 0, patch_k, whole)
+    whole = jnp.where((lane == 0) & (row == 0), both, whole)
+    bias_small[...] = jnp.where(row > SGRID * SGRID, NEGATIVE, whole)
+
+
+def attend_kernel(
+    n_small,
+    n_large,
+    large_seq,
+    small_seq,
+    edge,
+    query,
+    key,
+    value,
+    out,
+    out_wide,
+    probs_small,
+    probs_large,
+    wide,
+    narrow,
+    bias_large,
+    bias_small,
+):
+    masks = head_masks()
+
+    @pl.when(pl.program_id(0) == 0)
+    def _():
+        bias_small[...] = jnp.zeros_like(bias_small)
+
+    members = [(i * SPAD, SPAD, bias_small, probs_small, i) for i in range(n_small)]
+    members += [
+        (n_small * SPAD + i * LPAD, LPAD, bias_large, probs_large, i) for i in range(n_large)
+    ]
+    halves = [[] for _ in members]
+    for head in range(2):
+        transposed_biases(
+            large_seq[head], small_seq[head], edge[head], wide, narrow, bias_large, bias_small
+        )
+        for at, (start, count, bias, probs, which) in enumerate(members):
+            rows = pl.ds(start, count)
+            scores = dot_nt(key[rows, :], query[rows, :] * masks[head]) + bias[:, :count]
+            top = jnp.max(scores, axis=0, keepdims=True)
+            weights = jnp.exp(scores - top)
+            total = jnp.sum(weights, axis=0, keepdims=True)
+            prob = (weights * (1.0 / total)).astype(BF16)
+            probs[head, which] = prob
+            turned = value[rows, :].T
+            halves[at].append(dot_nn(turned[head * 64 : head * 64 + 64, :], prob))
+    for at, (start, count, bias, probs, which) in enumerate(members):
+        both = jnp.concatenate(halves[at], axis=0).T
+        out[pl.ds(start, count), :] = both.astype(BF16)
+        out_wide[pl.ds(start, count), :] = both
+
+
+def attend_back_kernel(
+    n_small,
+    n_large,
+    query,
+    key,
+    value,
+    dout,
+    out_wide,
+    probs_small,
+    probs_large,
+    dquery,
+    dkey,
+    dvalue,
+    large_seq,
+    small_seq,
+    edge,
+    wide,
+    narrow,
+    dsum_small,
+    dscore_large,
+):
+    masks = head_masks()
+    lane = iota((1, LANES), 1)
+    scale = float(64) ** (-0.5)
+    members = [(i * SPAD, SPAD, probs_small, i) for i in range(n_small)]
+    members += [(n_small * SPAD + i * LPAD, LPAD, probs_large, i) for i in range(n_large)]
+    keep = []
+    for head in range(2):
+        spot = 64 * (1 - head)
+        minus = jnp.where((lane == spot) | (lane == spot + 1), -1.0, 0.0).astype(BF16)
+        mask32 = masks[head].astype(F32)
+        for at, (start, count, probs, which) in enumerate(members):
+            rows = pl.ds(start, count)
+            grad = dout[rows, :]
+            grad32 = grad.astype(F32) * mask32
+            delta = jnp.sum(grad32 * out_wide[rows, :], axis=1, keepdims=True)
+            coarse = delta.astype(BF16).astype(F32)
+            fine = delta - coarse
+            side = jnp.where(lane == spot, coarse, jnp.where(lane == spot + 1, fine, grad32))
+            values = value[rows, :] * masks[head] + minus
+            prob = probs[head, which]
+            dscore = prob.astype(F32) * dot_nt(values, side.astype(BF16))
+            if count == SPAD:
+                if which == 0:
+                    dsum_small[:, :SPAD] = dscore
+                else:
+                    dsum_small[:, :SPAD] += dscore
+            elif which == 0:
+                dscore_large[:, :LPAD] = dscore
+            else:
+                dscore_large[:, :LPAD] += dscore
+            low = dscore.astype(BF16)
+            turned = key[rows, :].T
+            dq = dot_nn(turned[head * 64 : head * 64 + 64, :], low)
+            dk = dot_nn(low, query[rows, :])
+            dv = dot_nn(prob, grad)
+            if head == 0:
+                keep.append((dq, dk, dv))
+            else:
+                first = iota((count, LANES), 1) < 64
+                dq0, dk0, dv0 = keep[at]
+                dquery[rows, :] = (jnp.concatenate([dq0, dq], axis=0).T * scale).astype(BF16)
+                dkey[rows, :] = jnp.where(first, dk0, dk).astype(BF16)
+                dvalue[rows, :] = jnp.where(first, dv0, dv).astype(BF16)
+        wide[...] = jnp.zeros_like(wide)
+        dscore_large[:, LPAD:] = jnp.zeros((LPAD, 768 - LPAD), F32)
+        edge_lane = iota((24, 768), 1)
+        edge_row = iota((24, 768), 0)
+        class_column = jnp.zeros((24, 768), F32)
+        class_row = None
+        for block in range(LGRID + 1):
+            at, turn = large_window(block)
+            piece = dscore_large[pl.ds(block * 24, 24), :]
+            if block == 0:
+                class_row = piece[0:1, :]
+                piece = jnp.where(edge_row == 0, 0.0, piece)
+            class_column = class_column + piece
+            piece = jnp.where(edge_lane == 0, 0.0, piece)
+            if turn:
+                piece = pltpu.roll(piece, turn, 1)
+            wide[:, at * LANES : at * LANES + 768] += piece
+        low_sum, high_sum = gather_sequences(wide[...], 24, L_WIDTH, LGRID, 1)
+        large_seq[head, 0:1, :] = low_sum
+        large_seq[head, 1:2, :] = high_sum
+        narrow[...] = jnp.zeros_like(narrow)
+        dsum_small[:, SPAD:] = jnp.zeros((SPAD, 384 - SPAD), F32)
+        small_lane = iota((SGRID, 384), 1)
+        small_column = jnp.zeros((SGRID, 384), F32)
+        for block in range(SGRID):
+            at, turn = small_window(block)
+            piece = dsum_small[pl.ds(1 + SGRID * block, SGRID), :]
+            small_column = small_column + piece
+            piece = jnp.where(small_lane == 0, 0.0, piece)
+            piece = jnp.concatenate([piece, jnp.zeros((2, 384), F32)], axis=0)
+            if turn:
+                piece = pltpu.roll(piece, turn, 1)
+            narrow[:, at * LANES : at * LANES + 384] += piece
+        low_sum, high_sum = gather_sequences(narrow[...], 16, S_WIDTH, SGRID, 0)
+        small_seq[head, 0:1, :] = low_sum
+        small_seq[head, 1:2, :] = high_sum
+        edge[head, 0:1, :] = row_sum(class_column)[:, :LANES] + row_sum(small_column)[:, :LANES]
+        both_rows = class_row + jnp.concatenate(
+            [dsum_small[0:1, :], jnp.zeros((1, 384), F32)], axis=1
+        )
+        edge[head, 1:2, :] = jnp.broadcast_to(
+            jnp.sum(jnp.where(iota((1, 768), 1) == 0, 0.0, both_rows), axis=1, keepdims=True),
+            (1, LANES),
+        )
+        edge[head, 2:3, :] = both_rows[:, :LANES]
+        edge[head, 3:8, :] = jnp.zeros((5, LANES), F32)
+
+
+def qkv_kernel(x, gain, bias, weight, weight_bias, out):
+    width = x.shape[1]
+    normal, unused = normalized(x[...].astype(F32))
+    hidden = (normal * gain[...] + bias[...]).astype(BF16)
+    scale = float(width // HEADS) ** (-0.5)
+    for part in range(3):
+        cols = slice(part * width, (part + 1) * width)
+        made = (dot_nn(hidden, weight[:, cols]) + weight_bias[:, cols]).astype(BF16)
+        out[:, cols] = made * jnp.asarray(scale, BF16) if part == 0 else made
+
+
+def gelu_pair(upper):
+    normal_cdf = 0.5 * (1.0 + lax.erf(upper * (0.5**0.5)))
+    density = jnp.exp(-0.5 * upper * upper) * 0.3989422804014327
+    return upper * normal_cdf, normal_cdf + upper * density
+
+
+def valid_rows(first, count, n_small):
+    row = iota((count, 1), 0) + first
+    in_small = row < n_small * SPAD
+    small_ok = row % SPAD < SGRID * SGRID + 1
+    large_ok = (row - n_small * SPAD) % LPAD < LGRID * LGRID + 1
+    return jnp.where(in_small, small_ok.astype(F32), large_ok.astype(F32))
+
+
+def feed_kernel(
+    n_small,
+    tiles,
+    x,
+    attended,
+    cot,
+    w_out,
+    w_up,
+    w_down,
+    vectors,
+    up_bias,
+    out,
+    dresidual,
+    dattended,
+    vector_grads,
+    up_bias_grad,
+    g_out,
+    g_up,
+    g_down,
+    active,
+    slope,
+    acc_out,
+    acc_up,
+    acc_down,
+    stage,
+    sems,
+):
+    step = pl.program_id(0)
+    count, width = x.shape
+    tile = w_up.shape[1] // tiles
+
+    @pl.when(step == 0)
+    def _():
+        acc_out[...] = jnp.zeros_like(acc_out)
+        acc_up[...] = jnp.zeros_like(acc_up)
+        acc_down[...] = jnp.zeros_like(acc_down)
+        vector_grads[...] = jnp.zeros_like(vector_grads)
+        up_bias_grad[...] = jnp.zeros_like(up_bias_grad)
+
+    out_bias = vectors[0:1, :]
+    attend_scale = vectors[1:2, :]
+    second_gain = vectors[2:3, :]
+    second_bias = vectors[3:4, :]
+    down_bias = vectors[4:5, :]
+    feed_scale = vectors[5:6, :]
+
+    valid = valid_rows(step * count, count, n_small)
+    mixed = attended[...]
+    branch = dot_nn(mixed, w_out[...]) + out_bias
+    residual = x[...].astype(F32) + attend_scale * branch
+    normal, scale = normalized(residual)
+    hidden = (normal * second_gain + second_bias).astype(BF16)
+    lower = jnp.zeros((count, width), F32)
+    for t in range(tiles):
+        cols = slice(t * tile, (t + 1) * tile)
+        upper = dot_nn(hidden, w_up[:, cols]) + up_bias[:, cols]
+        made, rate = gelu_pair(upper)
+        made = made.astype(BF16)
+        active[:, cols] = made
+        slope[:, cols] = rate.astype(BF16)
+        lower += dot_nn(made, w_down[cols, :])
+    lower += down_bias
+    out[...] = ((residual + feed_scale * lower) * valid).astype(BF16)
+    upstream = cot[...].astype(F32) * valid
+    vector_grads[5:6, :] += row_sum(upstream * lower)
+    dlower = (upstream * feed_scale).astype(BF16)
+    vector_grads[4:5, :] += row_sum(dlower.astype(F32))
+    turned = hidden.T
+    dhidden = jnp.zeros((count, width), F32)
+    for t in range(tiles):
+        cols = slice(t * tile, (t + 1) * tile)
+        dupper = (dot_nt(dlower, w_down[cols, :]) * slope[:, cols].astype(F32)).astype(BF16)
+        up_bias_grad[:, cols] += row_sum(dupper.astype(F32))
+        acc_down[cols, :] += dot_nn(active[:, cols].T, dlower)
+        acc_up[:, cols] += dot_nn(turned, dupper)
+        dhidden += dot_nt(dupper, w_up[:, cols])
+    vector_grads[2:3, :] += row_sum(dhidden * normal)
+    vector_grads[3:4, :] += row_sum(dhidden)
+    dres = upstream + norm_back(dhidden * second_gain, normal, scale)
+    dresidual[...] = dres
+    vector_grads[1:2, :] += row_sum(dres * branch)
+    dbranch = (dres * attend_scale).astype(BF16)
+    vector_grads[0:1, :] += row_sum(dbranch.astype(F32))
+    acc_out[...] += dot_nn(mixed.T, dbranch)
+    dattended[...] = dot_nt(dbranch, w_out[...]).astype(BF16)
+
+    @pl.when(step == pl.num_programs(0) - 1)
+    def _():
+        part = stage.shape[1]
+        jobs = [
+            (source, target, slice(r, r + part), slice(c, c + width))
+            for source, target in ((acc_out, g_out), (acc_up, g_up), (acc_down, g_down))
+            for r in range(0, source.shape[0], part)
+            for c in range(0, source.shape[1], width)
+        ]
+        flights = []
+        for at, (source, target, rows, cols) in enumerate(jobs):
+            slot = at % 2
+            if at >= 2:
+                flights[at - 2].wait()
+            stage[slot] = source[rows, cols].astype(BF16)
+            flight = pltpu.make_async_copy(stage.at[slot], target.at[rows, cols], sems.at[slot])
+            flight.start()
+            flights.append(flight)
+        for flight in flights[-2:]:
+            flight.wait()
+
+
+def input_kernel(
+    x, dquery, dkey, dvalue, dresidual, gain, bias, weight, out, vector_grads, grad, acc
+):
+    step = pl.program_id(0)
+    width = x.shape[1]
+
+    @pl.when(step == 0)
+    def _():
+        acc[...] = jnp.zeros_like(acc)
+        vector_grads[...] = jnp.zeros_like(vector_grads)
+
+    normal, scale = normalized(x[...].astype(F32))
+    hidden = (normal * gain[...] + bias[...]).astype(BF16)
+    turned = hidden.T
+    dhidden = jnp.zeros(normal.shape, F32)
+    for part, item in enumerate((dquery, dkey, dvalue)):
+        cols = slice(part * width, (part + 1) * width)
+        piece = item[...]
+        dhidden += dot_nt(piece, weight[:, cols])
+        acc[:, cols] += dot_nn(turned, piece)
+        if part != 1:
+            vector_grads[part : part + 1, :] += row_sum(piece.astype(F32))
+    vector_grads[3:4, :] += row_sum(dhidden * normal)
+    vector_grads[4:5, :] += row_sum(dhidden)
+    out[...] = (dresidual[...] + norm_back(dhidden * gain[...], normal, scale)).astype(BF16)
+
+    @pl.when(step == pl.num_programs(0) - 1)
+    def _():
+        grad[...] = acc[...].astype(BF16)
+
+
+def chunk_rows(total):
+    return max(size for size in range(16, 481, 16) if total % size == 0)
+
+
+def params():
+    return pltpu.CompilerParams(vmem_limit_bytes=VMEM_BYTES)
+
+
+def held(shape):
+    rank = len(shape)
+    return pl.BlockSpec(shape, lambda i: (0,) * rank, pipeline_mode=pl.Buffered(1))
+
+
+def resident(shape):
+    rank = len(shape)
+    return pl.BlockSpec(shape, lambda i: (0,) * rank)
+
+
+def run_qkv(x, gain, bias, weight, weight_bias):
+    rows, width = x.shape
+    size = chunk_rows(rows)
+    wide = weight.shape[1]
+    return pl.pallas_call(
+        qkv_kernel,
+        grid=(rows // size,),
+        in_specs=[
+            pl.BlockSpec((size, width), lambda i: (i, 0)),
+            held((1, width)),
+            held((1, width)),
+            held(weight.shape),
+            held((1, wide)),
+        ],
+        out_specs=pl.BlockSpec((size, wide), lambda i: (i, 0)),
+        out_shape=jax.ShapeDtypeStruct((rows, wide), BF16),
+        compiler_params=params(),
+        cost_estimate=pl.CostEstimate(
+            flops=2 * rows * width * wide, bytes_accessed=rows * wide * 2, transcendentals=0
+        ),
+    )(x, gain, bias, weight, weight_bias)
+
+
+def run_attend(qkv, large_seq, small_seq, edge, n_small, n_large):
+    rows = qkv.shape[0]
+    width = qkv.shape[1] // 3
+    pairs = HEADS // 2
+
+    def column(which):
+        return pl.BlockSpec((rows, LANES), lambda i: (0, which * pairs + i))
+
+    def per_pair(shape):
+        tail = (0,) * (len(shape) - 1)
+        return pl.BlockSpec((2,) + shape[1:], lambda i: (i,) + tail)
+
+    return pl.pallas_call(
+        functools.partial(attend_kernel, n_small, n_large),
+        grid=(pairs,),
+        in_specs=[
+            per_pair(large_seq.shape),
+            per_pair(small_seq.shape),
+            per_pair(edge.shape),
+            column(0),
+            column(1),
+            column(2),
+        ],
+        out_specs=[
+            column(0),
+            column(0),
+            per_pair((HEADS, n_small, SPAD, SPAD)),
+            per_pair((HEADS, n_large, LPAD, LPAD)),
+        ],
+        out_shape=[
+            jax.ShapeDtypeStruct((rows, width), BF16),
+            jax.ShapeDtypeStruct((rows, width), F32),
+            jax.ShapeDtypeStruct((HEADS, n_small, SPAD, SPAD), BF16),
+            jax.ShapeDtypeStruct((HEADS, n_large, LPAD, LPAD), BF16),
+        ],
+        scratch_shapes=[
+            pltpu.VMEM((24, L_WIDTH), F32),
+            pltpu.VMEM((16, S_WIDTH), F32),
+            pltpu.VMEM((LPAD, 640), F32),
+            pltpu.VMEM((SPAD, 256), F32),
+        ],
+        compiler_params=params(),
+        cost_estimate=pl.CostEstimate(
+            flops=20 * 10**9, bytes_accessed=20 * 10**6, transcendentals=7 * 10**6
+        ),
+    )(large_seq, small_seq, edge, qkv, qkv, qkv)
+
+
+def run_attend_back(qkv, dattended, out_wide, probs_small, probs_large, n_small, n_large):
+    rows, width = dattended.shape
+    pairs = HEADS // 2
+
+    def column(which):
+        return pl.BlockSpec((rows, LANES), lambda i: (0, which * pairs + i))
+
+    def per_pair(shape):
+        tail = (0,) * (len(shape) - 1)
+        return pl.BlockSpec((2,) + shape[1:], lambda i: (i,) + tail)
+
+    grad = jax.ShapeDtypeStruct((rows, width), BF16)
+    return pl.pallas_call(
+        functools.partial(attend_back_kernel, n_small, n_large),
+        grid=(pairs,),
+        in_specs=[
+            column(0),
+            column(1),
+            column(2),
+            column(0),
+            column(0),
+            per_pair(probs_small.shape),
+            per_pair(probs_large.shape),
+        ],
+        out_specs=[
+            column(0),
+            column(0),
+            column(0),
+            per_pair((HEADS, 2, L_WIDTH)),
+            per_pair((HEADS, 2, S_WIDTH)),
+            per_pair((HEADS, 8, LANES)),
+        ],
+        out_shape=[
+            grad,
+            grad,
+            grad,
+            jax.ShapeDtypeStruct((HEADS, 2, L_WIDTH), F32),
+            jax.ShapeDtypeStruct((HEADS, 2, S_WIDTH), F32),
+            jax.ShapeDtypeStruct((HEADS, 8, LANES), F32),
+        ],
+        scratch_shapes=[
+            pltpu.VMEM((24, L_WIDTH), F32),
+            pltpu.VMEM((16, S_WIDTH), F32),
+            pltpu.VMEM((SPAD, 384), F32),
+            pltpu.VMEM((LPAD, 768), F32),
+        ],
+        compiler_params=params(),
+        cost_estimate=pl.CostEstimate(
+            flops=30 * 10**9, bytes_accessed=24 * 10**6, transcendentals=0
+        ),
+    )(qkv, qkv, qkv, dattended, out_wide, probs_small, probs_large)
+
+
+def run_feed(x, attended, cot, w_out, w_up, w_down, vectors, up_bias, n_small):
+    rows, width = x.shape
+    size = chunk_rows(rows)
+    hidden = w_up.shape[1]
+    tiles = hidden // width
+    block = pl.BlockSpec((size, width), lambda i: (i, 0))
+    anywhere = pl.BlockSpec(memory_space=pl.ANY)
+    return pl.pallas_call(
+        functools.partial(feed_kernel, n_small, tiles),
+        grid=(rows // size,),
+        in_specs=[
+            block,
+            block,
+            block,
+            held(w_out.shape),
+            held(w_up.shape),
+            held(w_down.shape),
+            held(vectors.shape),
+            held(up_bias.shape),
+        ],
+        out_specs=[
+            block,
+            block,
+            block,
+            resident((8, width)),
+            resident((1, hidden)),
+            anywhere,
+            anywhere,
+            anywhere,
+        ],
+        out_shape=[
+            jax.ShapeDtypeStruct((rows, width), BF16),
+            jax.ShapeDtypeStruct((rows, width), F32),
+            jax.ShapeDtypeStruct((rows, width), BF16),
+            jax.ShapeDtypeStruct((8, width), F32),
+            jax.ShapeDtypeStruct((1, hidden), F32),
+            jax.ShapeDtypeStruct((width, width), BF16),
+            jax.ShapeDtypeStruct((width, hidden), BF16),
+            jax.ShapeDtypeStruct((hidden, width), BF16),
+        ],
+        scratch_shapes=[
+            pltpu.VMEM((size, hidden), BF16),
+            pltpu.VMEM((size, hidden), BF16),
+            pltpu.VMEM((width, width), F32),
+            pltpu.VMEM((width, hidden), F32),
+            pltpu.VMEM((hidden, width), F32),
+            pltpu.VMEM((2, width // 4, width), BF16),
+            pltpu.SemaphoreType.DMA((2,)),
+        ],
+        compiler_params=params(),
+        cost_estimate=pl.CostEstimate(
+            flops=6 * rows * width * (width + 2 * hidden),
+            bytes_accessed=40 * 10**6,
+            transcendentals=2 * rows * hidden,
+        ),
+    )(x, attended, cot, w_out, w_up, w_down, vectors, up_bias)
+
+
+def run_input(x, dquery, dkey, dvalue, dresidual, gain, bias, weight):
+    rows, width = x.shape
+    size = chunk_rows(rows)
+    block = pl.BlockSpec((size, width), lambda i: (i, 0))
+    return pl.pallas_call(
+        input_kernel,
+        grid=(rows // size,),
+        in_specs=[
+            block,
+            block,
+            block,
+            block,
+            block,
+            held((1, width)),
+            held((1, width)),
+            held(weight.shape),
+        ],
+        out_specs=[block, resident((8, width)), resident(weight.shape)],
+        out_shape=[
+            jax.ShapeDtypeStruct((rows, width), BF16),
+            jax.ShapeDtypeStruct((8, width), F32),
+            jax.ShapeDtypeStruct(weight.shape, BF16),
+        ],
+        scratch_shapes=[pltpu.VMEM(weight.shape, F32)],
+        compiler_params=params(),
+        cost_estimate=pl.CostEstimate(
+            flops=12 * rows * width * width, bytes_accessed=20 * 10**6, transcendentals=0
+        ),
+    )(x, dquery, dkey, dvalue, dresidual, gain, bias, weight)
 
 
 def shifted(array, axis, by):
@@ -283,7 +1010,7 @@
     return (carry[0], send_grads(carry[1]), carry[2])
 
 
-def per_device(
+def general_device(
     small_in,
     large_in,
     small_cot,
@@ -491,6 +1218,152 @@
     )
 
 
+def exchange_large(part):
+    position = lax.axis_index("seq")
+    stay = lax.dynamic_index_in_dim(part, position, 0, keepdims=False)
+    leave = lax.dynamic_index_in_dim(part, 1 - position, 0, keepdims=False)
+    came = shifted(leave, "seq", 1)
+    return jnp.where(
+        position == 0,
+        jnp.concatenate([stay, came], axis=0),
+        jnp.concatenate([came, stay], axis=0),
+    )
+
+
+def return_large(whole, rows):
+    position = lax.axis_index("seq")
+    stay = lax.dynamic_slice_in_dim(whole, position * rows, rows, 0)
+    leave = lax.dynamic_slice_in_dim(whole, (1 - position) * rows, rows, 0)
+    came = shifted(leave, "seq", 1)
+    return jnp.where(position == 0, jnp.stack([stay, came]), jnp.stack([came, stay]))
+
+
+def image_device(
+    small_in,
+    large_in,
+    small_cot,
+    large_cot,
+    first_gain,
+    first_bias,
+    query_weight,
+    query_bias,
+    key_weight,
+    value_weight,
+    value_bias,
+    out_weight,
+    out_bias,
+    attend_scale,
+    second_gain,
+    second_bias,
+    up_weight,
+    up_bias,
+    down_weight,
+    down_bias,
+    feed_scale,
+    rel_table,
+):
+    groups, small_rows, width = small_in.shape
+    large_rows = large_in.shape[1]
+    n_small = groups * small_rows // SLEN
+    n_large = 1
+    small_part = n_small * SPAD
+
+    def compact(small, large):
+        return jnp.concatenate(
+            [
+                small.reshape(n_small, SLEN, width)[:, :SPAD].reshape(small_part, width),
+                exchange_large(large)[:LPAD],
+            ],
+            axis=0,
+        )
+
+    def expand_small(rows):
+        small = rows[:small_part].reshape(n_small, SPAD, width)
+        small = jnp.pad(small, ((0, 0), (0, SLEN - SPAD), (0, 0)))
+        return small.reshape(groups, small_rows, width)
+
+    def expand_large(rows):
+        large = jnp.pad(rows[small_part:], ((0, LLEN - LPAD), (0, 0)))
+        return return_large(large, large_rows)
+
+    qkv_share = jnp.concatenate([query_weight, key_weight, value_weight], axis=1)
+    w_qkv = lax.all_gather(qkv_share, "img", axis=0, tiled=True)
+    mid_share = jnp.concatenate([out_weight, up_weight], axis=1)
+    w_mid = lax.all_gather(mid_share, "img", axis=0, tiled=True)
+    w_out, w_up = w_mid[:, :width], w_mid[:, width:]
+    w_down = lax.all_gather(down_weight, "img", axis=0, tiled=True)
+
+    large_seq, small_seq, edge = table_sequences(rel_table)
+    x = compact(small_in, large_in)
+    cot = compact(small_cot, large_cot)
+    gain, bias = first_gain[None], first_bias[None]
+    qkv_bias = jnp.concatenate([query_bias, jnp.zeros_like(query_bias), value_bias])[None]
+    vectors = jnp.stack(
+        [out_bias, attend_scale, second_gain, second_bias, down_bias, feed_scale]
+        + [feed_scale] * 2
+    )
+
+    qkv = run_qkv(x, gain, bias, w_qkv, qkv_bias)
+    attended, out_wide, probs_small, probs_large = run_attend(
+        qkv, large_seq, small_seq, edge, n_small, n_large
+    )
+    out, dresidual, dattended, vector_grads, up_bias_grad, g_out, g_up, g_down = run_feed(
+        x, attended, cot, w_out, w_up, w_down, vectors, up_bias[None], n_small
+    )
+    small_out, large_out = expand_small(out), expand_large(out)
+
+    def reduce(share):
+        share = lax.psum_scatter(share, "img", scatter_dimension=0, tiled=True)
+        return lax.psum(share.astype(F32), "seq")
+
+    g_mid = reduce(jnp.concatenate([g_out, g_up], axis=1))
+    g_down = reduce(g_down)
+    dquery, dkey, dvalue, d_large, d_small, d_edge = run_attend_back(
+        qkv, dattended, out_wide, probs_small, probs_large, n_small, n_large
+    )
+    dinput, input_grads, g_qkv = run_input(
+        x, dquery, dkey, dvalue, dresidual, gain, bias, w_qkv
+    )
+    small_grad, large_grad = expand_small(dinput), expand_large(dinput)
+    g_qkv = reduce(g_qkv)
+    edge_grad = jnp.stack([d_edge[:, 0, 0], d_edge[:, 1, 0], d_edge[:, 2, 0]], axis=1)
+    vector_grads, up_bias_grad, input_grads, d_large, d_small, edge_grad = lax.psum(
+        (vector_grads, up_bias_grad, input_grads, d_large, d_small, edge_grad), ("img", "seq")
+    )
+    table_grad = table_from_sequences(d_large, d_small, edge_grad)
+    return (
+        small_out,
+        large_out,
+        small_grad,
+        large_grad,
+        input_grads[3],
+        input_grads[4],
+        g_qkv[:, :width],
+        input_grads[0],
+        g_qkv[:, width : 2 * width],
+        g_qkv[:, 2 * width :],
+        input_grads[2],
+        g_mid[:, :width],
+        vector_grads[0],
+        vector_grads[1],
+        vector_grads[2],
+        vector_grads[3],
+        g_mid[:, width:],
+        up_bias_grad[0],
+        g_down,
+        vector_grads[4],
+        vector_grads[5],
+        table_grad,
+    )
+
+
+def per_device(*args):
+    groups, small_rows, unused = args[0].shape
+    if lax.axis_size("seq") == 2 and groups == 2 and small_rows % SLEN == 0:
+        return image_device(*args)
+    return general_device(*args)
+
+
 def solution(mesh):
     return jax.shard_map(
         per_device,

time: 1880 us -> 859 us (0.46)
  matrix products: 942 us -> 0 us
  local copies, waits for them, and re-layouts: 403 us -> 38.8 us
  waiting for transfers between devices: 336 us -> 555 us
  Pallas kernels: 0 us -> 163 us
  other arithmetic: 116 us -> 22.7 us
    dot_general x60 -> x0, matrix products: 942 us -> none  [the longest x4 181 us: position_bias(): jnp.einsum('qar,hqac->hqrc', row_hot, partial_bias, precision=lax.Precisi...]
    reduce_scatter x6 -> x3, waiting for transfers between devices: 0.04 us -> 230 us  [reduce(): share = lax.psum_scatter(share, 'img', scatter_dimension=0, tiled=True)]
    ppermute x6 -> x4, waiting for transfers between devices: 222 us -> 4.28 us  [shifted(): lax.ppermute(array, axis, [(i, (i + by) % count) for i in range(count)])]
    pallas_call x0 -> x5, Pallas kernels: none -> 163 us  [the longest x1 76.7 us: run_feed(): pl.pallas_call(functools.partial(feed_kernel, n_small, tiles), grid=(rows...]
    transpose x4 -> x0, local copies, waits for them, and re-layouts: 160 us -> none  [the longest x2 88.3 us: position_bias(): jnp.einsum('hab,qbc->hqac', grid_table, col_hot, precision=lax.Precision....]
    reshape x16 -> x6, local copies, waits for them, and re-layouts: 130 us -> 0.99 us  [the longest x2 0.3 us: sequences(): jnp.pad(part[:, :, grid:], ((0, 0), (0, 0), (0, 1)))]
    psum x2, waiting for transfers between devices: 110 us -> 229 us  [image_device(): lax.psum((vector_grads, up_bias_grad, input_grads, d_large, d_small, edge...]
    all_gather x6 -> x3, waiting for transfers between devices: 0.03 us -> 89.2 us  [the longest x1 47.1 us: image_device(): w_down = lax.all_gather(down_weight, 'img', axis=0, tiled=True)]
  transfers between devices with their start and end apart: 20 -> 12, of which waited for: 5 -> 9; matrix products, arithmetic and copies ran while one was open for 65% -> 6% of each run, Pallas kernels for 0% -> 4%
where the time goes in v1:
time: 859 us; the launch traced here: 845 us
  waiting for transfers between devices  555 us (65%)
  Pallas kernels  163 us (19%)
  blocking collectives  44.7 us (5%)
  local copies, waits for them, and re-layouts  38.8 us (5%)
  other arithmetic  22.7 us (3%)
  between operations  14.7 us (2%)
    reduce_scatter x3, waiting for transfers between devices, reduce(): share = lax.psum_scatter(share, 'img', scatter_dimension=0, tiled=True)  230 us
    psum x2, waiting for transfers between devices, image_device(): lax.psum((vector_grads, up_bias_grad, input_grads, d_large, d_small, edge...  229 us
    pallas_call x1, Pallas kernels, run_feed(): pl.pallas_call(functools.partial(feed_kernel, n_small, tiles), grid=(rows...  76.7 us
    all_gather x1, waiting for transfers between devices, image_device(): w_down = lax.all_gather(down_weight, 'img', axis=0, tiled=True)  47.1 us
    psum x1, blocking collectives, reduce(): return lax.psum(share.astype(F32), 'seq')  44.7 us
    pallas_call x1, Pallas kernels, run_attend_back(): pl.pallas_call(functools.partial(attend_back_kernel, n_small, n_large), g...  29.2 us
    pallas_call x1, Pallas kernels, run_attend(): pl.pallas_call(functools.partial(attend_kernel, n_small, n_large), grid=(...  26.8 us
    all_gather x1, waiting for transfers between devices, image_device(): w_mid = lax.all_gather(mid_share, 'img', axis=0, tiled=True)  23.8 us
  transfers between devices with their start and end apart: 12, of which 9 were waited for; matrix products, arithmetic and copies ran while one was open for 6% of the time, Pallas kernels for 4%

profile of v1, /device:TPU:0, one launch (start us, length us, event | category | flops | bytes accessed | tf_op | source)
XLA Modules:
  0.0 844.5 jit_solution(13453115176682141276)
XLA Ops:
  7.3 1.8 pad_maximum_fusion.8
  9.1 1.7 pad_maximum_fusion.7
  11.0 0.7 all-gather.8.cloned.1.call-update
  11.7 0.8 dynamic-slice_bitcast_fusion.3
  12.6 3.0 collective-permute-start
  15.7 0.8 dynamic-slice_bitcast_fusion.1
  17.2 0.6 broadcast_in_dim.22.gain
  17.8 0.6 broadcast_in_dim.23.bias
  18.4 0.6 stack.79
  19.0 0.6 stack.80
  19.6 0.6 stack.81
  20.8 0.6 broadcast_in_dim.25.weight_bias
  21.6 0.7 stack.72
  22.5 0.6 stack.76
  23.5 0.7 stack.73
  24.2 0.6 stack.75
  24.8 1.4 slice.163
  26.2 1.4 slice.168
  27.6 1.4 stack.84.vectors
  29.0 1.4 pad_maximum_fusion.11.small_seq
  30.4 1.6 pad_maximum_fusion.10.large_seq
  32.0 1.4 fusion.1
  33.5 4.3 collective-permute-done.1
  37.7 1.5 fusion
  39.2 1.5 pad_maximum_fusion.1.x
  40.7 1.5 pad_maximum_fusion.2.cot
  42.2 18.4 %all-gather.4.cloned.1.call-done.weight = bf16[768,2304]{1,0:T(8,128)(2,1)} async-done(((bf16[48,2304]{1,0:T(8,128)(2,1)}), bf16[768,2304]{1,0:T(8,128)(2,1)}) %all-gather.4.cloned.1.call-update) | async-done | bytes 3538960 | tf_op jit(solution)/shard_map/all_gather | solution.py:1290
  60.6 10.3 %shard_map.381.query.key.value = bf16[1440,2304]{1,0:T(8,128)(2,1)} custom-call(bf16[1440,768]{1,0:T(8,128)(2,1)} %pad_maximum_fusion.1.x, f32[1,768]{1,0:T(1,128)} %broadcast_in_dim.22.gain, f32[1,768]{1,0:T(1,128)} %broadcast_in_dim.23.bias, bf16[768,2304]{1,0:T(8,128)(2,1)} %all-gather.4.cloned.1.call-done.weight, f32[1,2304]{1,0:T(1,128)} %broadcast_in_dim.25.weight_bias), custom_call_target="tpu_custom_call" | custom-call | flops 5096079360 | bytes 6635520 | tf_op jit(solution)/shard_map/pallas_call | solution.py:535
  70.9 0.7 broadcast_in_dim.21.edge
  71.6 26.8 %shard_map.382 = (bf16[1440,768]{1,0:T(8,128)(2,1)}, f32[1440,768]{1,0:T(8,128)}, bf16[12,4,208,208]{3,2,1,0:T(8,128)(2,1)}, bf16[12,1,608,608]{3,2,1,0:T(8,128)(2,1)}) custom-call(f32[12,2,1280]{2,1,0:T(2,128)} %pad_maximum_fusion.10.large_seq, f32[12,2,512]{2,1,0:T(2,128)} %pad_maximum_fusion.11.small_seq, f32[12,8,128]{2,1,0:T(8,128)} %broadcast_in_dim.21.edge, ...), custom_call_target="tpu_custom_call" | custom-call | flops 20000000000 | bytes 20000000 | tf_op jit(solution)/shard_map/pallas_call | solution.py:566
  98.4 23.8 %all-gather.6.cloned.1.call-done = bf16[768,3840]{1,0:T(8,128)(2,1)} async-done(((bf16[48,3840]{1,0:T(8,128)(2,1)}), bf16[768,3840]{1,0:T(8,128)(2,1)}) %all-gather.6.cloned.1.call-update) | async-done | bytes 5898256 | tf_op jit(solution)/shard_map/all_gather | solution.py:1292
  122.2 2.4 slice.169.w_out
  124.6 4.8 slice.170.w_up
  129.3 47.1 %all-gather.8.cloned.1.call-done.w_down = bf16[3072,768]{1,0:T(8,128)(2,1)} async-done(((bf16[192,768]{1,0:T(8,128)(2,1)}), bf16[3072,768]{1,0:T(8,128)(2,1)}) %all-gather.8.cloned.1.call-update) | async-done | bytes 4718608 | tf_op jit(solution)/shard_map/all_gather | solution.py:1294
  176.4 76.7 %shard_map.383 = (bf16[1440,768]{1,0:T(8,128)(2,1)}, f32[1440,768]{1,0:T(8,128)}, bf16[1440,768]{1,0:T(8,128)(2,1)}, f32[8,768]{1,0:T(8,128)}, f32[1,3072]{1,0:T...) custom-call(bf16[1440,768]{1,0:T(8,128)(2,1)} %pad_maximum_fusion.1.x, ...), custom_call_target="tpu_custom_call" | custom-call | flops 45864714240 | bytes 40000000 | tf_op jit(solution)/shard_map/pallas_call | solution.py:662
  253.1 29.2 %shard_map.384 = (bf16[1440,768]{1,0:T(8,128)(2,1)}, bf16[1440,768]{1,0:T(8,128)(2,1)}, bf16[1440,768]{1,0:T(8,128)(2,1)}, f32[12,2,1280]{2,1,0:T(2,128)}, f32[12,2,512]{2,1,0:T(2,128)}, /*index=5*/f32[12,8,128]{2,1,0:T(8,128)}) custom-call(bf16[1440,2304]{1,0:T(8,128)(2,1)} %shard_map.381.query.key.value, bf16[1440,2304]{1,0:T(8,128)(2,1)} %shard_map.381.query.key.value, ...), custom_call_target="tpu_custom_call" | custom-call | flops 30000001024 | bytes 24000000 | tf_op jit(solution)/shard_map/pallas_call | solution.py:614
  282.3 1.1 slice_reduce_fusion.6
  283.3 0.6 pad_maximum_fusion.13
  283.9 19.9 %shard_map.385 = (bf16[1440,768]{1,0:T(8,128)(2,1)}, f32[8,768]{1,0:T(8,128)}, bf16[768,2304]{1,0:T(8,128)(2,1)}) custom-call(bf16[1440,768]{1,0:T(8,128)(2,1)} %pad_maximum_fusion.1.x, bf16[1440,768]{1,0:T(8,128)(2,1)} %get-tuple-element.49.dquery, bf16[1440,768]{1,0:T(8,128)(2,1)} %get-tuple-element.50.dkey, bf16[1440,768]{1,0:T(8,128)(2,1)} %get-tuple-element.51.dvalue, ...), custom_call_target="tpu_custom_call" | custom-call | flops 10192158720 | bytes 20000000 | tf_op jit(solution)/shard_map/pallas_call | solution.py:717
  305.0 0.7 reduce-scatter.8.cloned.1.call-update
  306.3 5.2 pad_maximum_fusion
  311.6 1.6 copy-done.1
  313.3 1.5 copy-done
  315.1 1.5 collective-permute-start.3
  316.6 1.2 pad.55
  317.9 1.2 pad.53
  319.1 0.9 fusion.2
  320.5 104.9 %all-reduce.20.cloned.1.call-done = (f32[8,768]{1,0:T(8,128)}, f32[8,768]{1,0:T(8,128)}, f32[3072]{0:T(1024)}, f32[12,3]{0,1:T(4,128)}, f32[12,2,512]{2,1,0:T(2,128)}) async-done(((f32[8,768]{1,0:T(8,128)}, f32[8,768]{1,0:T(8,128)}, f32[3072]{0:T(1024)}, f32[12,3]{0,1:T(4,128)}, f32[12,2,512]{2,1,0:T(2,128)}), (f32[8,768]{1,0:T(8,128)}, f32[8,768]{1,0:T(8,128)}, f32[3072]{0:T(1024)}, f32[12,3]{0,1:T(4,128)}, ...) | async-done | bytes 110752 | tf_op jit(solution)/shard_map/psum | solution.py:1330
  425.4 0.8 copy.45
  426.1 1.0 slice_reduce_fusion.3
  427.5 1.7 slice_reduce_fusion.7
  429.2 124.3 %all-reduce.18.cloned.1.call-done = f32[12,2,1280]{2,1,0:T(2,128)} async-done(((f32[12,2,1280]{2,1,0:T(2,128)}), f32[12,2,1280]{2,1,0:T(2,128)}) %all-reduce.18.cloned.1.call-update) | async-done | bytes 122896 | tf_op jit(solution)/shard_map/psum | solution.py:1330
  553.5 1.3 slice_reduce_fusion.1
  555.7 0.7 pad_maximum_fusion.9
  556.4 1.1 maximum_select_fusion.1
  557.5 2.3 maximum_select_fusion
  559.8 65.6 %reduce-scatter.4.cloned.1.call-done = bf16[48,2304]{1,0:T(8,128)(2,1)} async-done(((bf16[768,2304]{1,0:T(8,128)(2,1)}), bf16[48,2304]{1,0:T(8,128)(2,1)}) %reduce-scatter.4.cloned.1.call-update) | async-done | bytes 221200 | tf_op jit(solution)/shard_map/reduce_scatter | solution.py:1316
  625.5 78.3 %reduce-scatter.8.cloned.1.call-done = bf16[192,768]{1,0:T(8,128)(2,1)} async-done(((bf16[3072,768]{1,0:T(8,128)(2,1)}), bf16[192,768]{1,0:T(8,128)(2,1)}) %reduce-scatter.8.cloned.1.call-update) | async-done | bytes 294928 | tf_op jit(solution)/shard_map/reduce_scatter | solution.py:1316
  703.8 86.1 %reduce-scatter.6.cloned.1.call-done = bf16[48,3840]{1,0:T(8,128)(2,1)} async-done(((bf16[768,3840]{1,0:T(8,128)(2,1)}), bf16[48,3840]{1,0:T(8,128)(2,1)}) %reduce-scatter.6.cloned.1.call-update) | async-done | bytes 368656 | tf_op jit(solution)/shard_map/reduce_scatter | solution.py:1316
  789.9 44.7 %all-reduce.21 = (f32[48,2304]{1,0:T(8,128)S(1)}, f32[48,3840]{1,0:T(8,128)S(1)}, f32[192,768]{1,0:T(8,128)}) all-reduce(bf16[48,2304]{1,0:T(8,128)(2,1)} %reduce-scatter.4.cloned.1.call-done, bf16[48,3840]{1,0:T(8,128)(2,1)} %reduce-scatter.6.cloned.1.call-done, ...), channel_id=1, replica_groups=mesh['img'=16,'seq'=2] {'seq'}, use_global_device_ids=true, to_apply=%region_2.3 | all-reduce | flops 442368 | bytes 2654208 | tf_op jit(solution)/shard_map/psum | solution.py:1317
  834.6 0.7 slice.178
  835.2 0.9 slice.183
  836.1 0.8 fusion.8
  836.9 0.6 copy.58
  (83 shorter events, 6.3 us)
Async XLA Ops:
  7.2 4.5 copy-start.3
  7.2 8.5 %copy-start.4 = (bf16[2,320,768]{2,1,0:T(8,128)(2,1)S(1)}, bf16[2,320,768]{2,1,0:T(8,128)(2,1)}, u32[]{:S(2)}) copy-start(bf16[2,320,768]{2,1,0:T(8,128)(2,1)} %param.25) | copy-start | bytes 2949124
  7.2 53.4 %all-gather.4.cloned.1.call-start = ((), (), s32[]{:S(2)}) async-start(), calls=%async_computation.3 | async-start | bytes 3760128 | tf_op jit(solution)/shard_map/all_gather | solution.py:1290
  9.1 113.1 %all-gather.6.cloned.1.call-start = ((), (), s32[]{:S(2)}) async-start(), calls=%async_computation.4 | async-start | bytes 6266880 | tf_op jit(solution)/shard_map/all_gather | solution.py:1292
  10.9 5.7 copy-start.15
  10.9 5.7 copy-start.16
  10.9 5.7 copy-start.5
  10.9 165.5 %all-gather.8.cloned.1.call-start = ((), (), s32[]{:S(2)}) async-start(), calls=%async_computation.5 | async-start | bytes 5013504 | tf_op jit(solution)/shard_map/all_gather | solution.py:1294
  11.7 413.7 %all-reduce.20.cloned.1.call-start = ((), (), s32[]{:S(2)}) async-start(), calls=%async_computation.10 | async-start | bytes 225280 | tf_op jit(solution)/shard_map/psum | solution.py:1330
  12.6 4.7 copy-start.7
  12.6 5.3 copy-start.8
  12.6 5.8 copy-start.9
  12.6 5.8 copy-start.10
  12.6 6.4 copy-start.11
  12.6 7.0 copy-start.12
  12.6 7.6 copy-start.13
  12.6 8.1 copy-start.14
  12.6 19.4 %collective-permute-start = (bf16[320,768]{1,0:T(8,128)(2,1)}, bf16[320,768]{1,0:T(8,128)(2,1)}, u32[]{:S(2)}, u32[]{:S(2)}) collective-permute-start(bf16[320,768]{1,0:T(8,128)(2,1)} %get-tuple-element.92), channel_id=1, source_target_pairs={{0,1},{1,0},{2,3},{3,2},{4,5},{5,4},{6,7},{7,6},{8,9},{9,8},{10,11... | collective-permute-start | bytes 1474568 | tf_op jit(solution)/shard_map/ppermute | solution.py:746
  16.5 21.2 %collective-permute-start.1 = (bf16[320,768]{1,0:T(8,128)(2,1)}, bf16[320,768]{1,0:T(8,128)(2,1)}, u32[]{:S(2)}, u32[]{:S(2)}) collective-permute-start(bf16[320,768]{1,0:T(8,128)(2,1)} %get-tuple-element.90), channel_id=1, source_target_pairs={{0,1},{1,0},{2,3},{3,2},{4,5},{5,4},{6,7},{7,6},{8,9},{9,8},{10,11... | collective-permute-start | bytes 1474568 | tf_op jit(solution)/shard_map/ppermute | solution.py:746
  303.8 249.7 %all-reduce.18.cloned.1.call-start = ((), (), s32[]{:S(2)}) async-start(), calls=%async_computation.9 | async-start | bytes 245760 | tf_op jit(solution)/shard_map/psum | solution.py:1330
  304.4 321.1 %reduce-scatter.4.cloned.1.call-start = ((), (), s32[]{:S(2)}) async-start(), calls=%async_computation.6 | async-start | bytes 3760128 | tf_op jit(solution)/shard_map/reduce_scatter | solution.py:1316
  305.0 398.8 %reduce-scatter.8.cloned.1.call-start = ((), (), s32[]{:S(2)}) async-start(), calls=%async_computation.8 | async-start | bytes 5013504 | tf_op jit(solution)/shard_map/reduce_scatter | solution.py:1316
  305.0 1.3 copy-start.2
  305.7 484.1 %reduce-scatter.6.cloned.1.call-start = ((), (), s32[]{:S(2)}) async-start(), calls=%async_computation.7 | async-start | bytes 6266880 | tf_op jit(solution)/shard_map/reduce_scatter | solution.py:1316
  311.6 1.6 copy-start.1
  313.2 1.6 copy-start
  315.1 241.3 %collective-permute-start.3 = (bf16[320,768]{1,0:T(8,128)(2,1)S(1)}, bf16[320,768]{1,0:T(8,128)(2,1)S(1)}, u32[]{:S(2)}, u32[]{:S(2)}) collective-permute-start(bf16[320,768]{1,0:T(8,128)(2,1)S(1)} %get-tuple-element.94), channel_id=1, source_target_pairs={{0,1},{1,0},{2,3},{3,2},{4,5},{5,4},{6,7},{7,6},{8,9},{9,8},{10,11... | collective-permute-start | bytes 1474568 | tf_op jit(solution)/shard_map/ppermute | solution.py:746
  320.0 237.6 %collective-permute-start.2 = (bf16[320,768]{1,0:T(8,128)(2,1)}, bf16[320,768]{1,0:T(8,128)(2,1)}, u32[]{:S(2)}, u32[]{:S(2)}) collective-permute-start(bf16[320,768]{1,0:T(8,128)(2,1)} %get-tuple-element.96), channel_id=1, source_target_pairs={{0,1},{1,0},{2,3},{3,2},{4,5},{5,4},{6,7},{7,6},{8,9},{9,8},{10,11... | collective-permute-start | bytes 1474568 | tf_op jit(solution)/shard_map/ppermute | solution.py:746
  557.5 279.3 %copy-start.6 = (f32[3072]{0:T(1024)S(1)}, f32[3072]{0:T(1024)}, u32[]{:S(2)}) copy-start(f32[3072]{0:T(1024)} %get-tuple-element.121) | copy-start | bytes 36868
Sparse Core Ops, SparseCore 0:
  10.9 49.6 all-gather.3
  63.4 58.7 all-gather.5
  124.5 51.8 all-gather.7
  303.9 121.3 all-reduce.19
  431.3 122.1 all-reduce.17
  557.2 68.1 reduce-scatter.3
  629.3 74.4 reduce-scatter.7
  708.3 81.5 reduce-scatter.5
